TPU v7x, 32 devices: a whole 2x2x4 slice. The times are simulated.
32 devices in a mesh: ctx: 16 (over z, y, x), head: 2 (over core).
Axes of the slice: x: 2, y: 2, z: 4, core: 2. Of those that a mesh axis runs over, the one named last changes fastest.
Arguments:
- content_rows: bfloat16 [4, 128, 4, 2048], P(None, 'ctx'), may hold values from -6 to 6
- w_hidden: bfloat16 [2048, 4096], P(None, 'head'), may hold values from -0.125 to 0.125
- w_embed: bfloat16 [4096, 512], P('head'), may hold values from -0.09375 to 0.09375
- w_query: bfloat16 [512, 512], P(None, 'head'), may hold values from -0.25 to 0.25
- w_gate: bfloat16 [512, 512], P(None, 'head'), may hold values from -0.25 to 0.25
- w_proj: bfloat16 [512, 512], P('head'), may hold values from -0.25 to 0.25
- history_keys: bfloat16 [4, 36864, 512], P(None, 'ctx', 'head'), may hold values from -6 to 6
- history_values: bfloat16 [4, 36864, 512], P(None, 'ctx', 'head'), may hold values from -6 to 6
- cutoffs: int32 [4, 128], replicated, may hold values from 9216 to 36864
- out_cotangent: bfloat16 [4, 128, 512], P(None, 'ctx'), may hold values from -6 to 6
Outputs:
- content_grad: bfloat16 [4, 128, 4, 2048], P(None, 'ctx', 'head')
Inputs may be any that keep to these rules, and one draw needn't show every extreme that they name: cutoffs[u, t] counts the leading events of user u's history that its target t sees.
All inputs are finite; a program needn't handle non-finite values.
Results may differ from a plain program's by a relative error of at most 0.02.
Values may be sent and summed in bfloat16 or wider, within the bound.
No kernel may reach another device: no remote copies, remote signals or barrier semaphores. Data moves between devices by JAX's collectives and lax.ppermute only.
A program may use at most 128 MiB of HBM per device.

v0:
```python
import jax
import jax.numpy as jnp
from jax import lax
from jax.sharding import PartitionSpec as P

DH = 128


def silu_slope(values_in):
    sigmoid_part = jax.nn.sigmoid(values_in)
    return sigmoid_part * (1.0 + values_in * (1.0 - sigmoid_part))


def contract_last(left, right):
    return lax.dot_general(
        left, right, (((1,), (1,)), ((), ())), preferred_element_type=jnp.float32
    )


def norm_grads(attended, gates, out_grad, heads_here):
    lead = attended.shape[:-1]
    attn_heads = attended.reshape(lead + (heads_here, DH))
    rscale = lax.rsqrt(jnp.mean(attn_heads * attn_heads, axis=-1, keepdims=True) + 1e-06)
    normed = attn_heads * rscale
    grad_heads = out_grad.reshape(lead + (heads_here, DH)).astype(jnp.float32)
    gate_heads = gates.reshape(lead + (heads_here, DH)).astype(jnp.float32)
    gate_grad = (grad_heads * normed).reshape(attended.shape)
    normed_grad = grad_heads * gate_heads
    attn_grad = rscale * (
        normed_grad - normed * jnp.mean(normed_grad * normed, axis=-1, keepdims=True)
    )
    return (attn_grad.reshape(attended.shape).astype(jnp.bfloat16), gate_grad)


def body(
    content_rows,
    w_hidden,
    w_embed,
    w_query,
    w_gate,
    w_proj,
    history_keys,
    history_values,
    cutoffs,
    out_cotangent,
):
    user_count, shard_rows, rows_each, width_in = content_rows.shape
    half_hidden = w_hidden.shape[1]
    model_width = w_query.shape[0]
    local_width = w_query.shape[1]
    heads_here = local_width // DH
    events = history_keys.shape[1]
    target_rows = user_count * shard_rows
    hidden_lin = jnp.dot(
        content_rows.reshape(-1, width_in), w_hidden, preferred_element_type=jnp.float32
    )
    hidden = jax.nn.silu(hidden_lin).astype(jnp.bfloat16)
    encoded = jnp.dot(hidden, w_embed, preferred_element_type=jnp.float32)
    summed = lax.psum(jnp.sum(encoded.reshape(target_rows, rows_each, model_width), axis=1), "head")
    embedded = (0.5 * summed).astype(jnp.bfloat16)
    query_lin = jnp.dot(embedded, w_query, preferred_element_type=jnp.float32)
    gate_lin = jnp.dot(embedded, w_gate, preferred_element_type=jnp.float32)
    queries = (
        jax.nn.silu(query_lin).astype(jnp.bfloat16).reshape(user_count, shard_rows, local_width)
    )
    gates = jax.nn.silu(gate_lin).astype(jnp.bfloat16).reshape(user_count, shard_rows, local_width)
    out_grad = contract_last(out_cotangent.reshape(-1, model_width), w_proj).astype(jnp.bfloat16)
    out_grad = out_grad.reshape(user_count, shard_rows, local_width)
    score_scale = DH ** (-0.5)
    positions = lax.axis_index("ctx") * events + jnp.arange(events, dtype=jnp.int32)
    key_heads = history_keys.reshape(user_count, events, heads_here, DH)
    value_heads = history_values.reshape(user_count, events, heads_here, DH)

    def forward_user(packed):
        user_queries, limits, user_keys, user_values = packed
        row_count = user_queries.shape[0]
        scores = (
            jnp.einsum(
                "thd,phd->htp",
                user_queries.reshape(row_count, heads_here, DH),
                user_keys,
                preferred_element_type=jnp.float32,
            )
            * score_scale
        )
        visible = positions[None, :] < limits[:, None]
        weights = jnp.where(visible[None], jax.nn.silu(scores), 0.0).astype(jnp.bfloat16)
        summed_rows = jnp.einsum(
            "htp,phd->thd", weights, user_values, preferred_element_type=jnp.float32
        )
        return summed_rows.reshape(row_count, local_width)

    queries_all = lax.all_gather(queries, "ctx", axis=1, tiled=True)
    partial_value = lax.map(forward_user, (queries_all, cutoffs, key_heads, value_heads))
    attended = lax.psum_scatter(partial_value, "ctx", scatter_dimension=1, tiled=True)
    attn_grad, gate_grad = norm_grads(attended, gates, out_grad, heads_here)
    grads_all = lax.all_gather(attn_grad, "ctx", axis=1, tiled=True)

    def backward_user(packed):
        user_queries, limits, user_keys, user_values, user_grads = packed
        row_count = user_queries.shape[0]
        scores = (
            jnp.einsum(
                "thd,phd->htp",
                user_queries.reshape(row_count, heads_here, DH),
                user_keys,
                preferred_element_type=jnp.float32,
            )
            * score_scale
        )
        visible = positions[None, :] < limits[:, None]
        weight_grad = jnp.einsum(
            "thd,phd->htp",
            user_grads.reshape(row_count, heads_here, DH),
            user_values,
            preferred_element_type=jnp.float32,
        )
        grad_scores = jnp.where(visible[None], weight_grad * silu_slope(scores), 0.0).astype(
            jnp.bfloat16
        )
        summed_rows = jnp.einsum(
            "htp,phd->thd", grad_scores, user_keys, preferred_element_type=jnp.float32
        )
        return summed_rows.reshape(row_count, local_width) * score_scale

    query_partial = lax.map(
        backward_user, (queries_all, cutoffs, key_heads, value_heads, grads_all)
    )
    query_grad = lax.psum_scatter(query_partial, "ctx", scatter_dimension=1, tiled=True)
    query_back = (query_grad.reshape(-1, local_width) * silu_slope(query_lin)).astype(jnp.bfloat16)
    gate_back = (gate_grad.reshape(-1, local_width) * silu_slope(gate_lin)).astype(jnp.bfloat16)
    embed_part = contract_last(query_back, w_query) + contract_last(gate_back, w_gate)
    embed_grad = (
        0.5 * lax.psum(embed_part.astype(jnp.bfloat16), "head").astype(jnp.float32)
    ).astype(jnp.bfloat16)
    hidden_grad = contract_last(embed_grad, w_embed)
    slopes = silu_slope(hidden_lin).reshape(target_rows, rows_each, half_hidden)
    hidden_back = (hidden_grad[:, None, :] * slopes).astype(jnp.bfloat16).reshape(-1, half_hidden)
    content_part = contract_last(hidden_back, w_hidden).reshape(
        user_count, shard_rows, rows_each, width_in
    )
    return lax.psum_scatter(
        content_part.astype(jnp.bfloat16), "head", scatter_dimension=2, tiled=True
    )


def solution(mesh):
    in_specs = (
        P(None, "ctx", None, None),
        P(None, "head"),
        P("head", None),
        P(None, "head"),
        P(None, "head"),
        P("head", None),
        P(None, "ctx", "head"),
        P(None, "ctx", "head"),
        P(),
        P(None, "ctx", None),
    )
    out_specs = P(None, "ctx", "head", None)
    return jax.shard_map(body, mesh=mesh, in_specs=in_specs, out_specs=out_specs, check_vma=False)
```

profile of v0, /device:TPU:0, one launch (start us, length us, event | category | flops | bytes accessed | tf_op | source)
XLA Modules:
  0.0 440.8 jit_solution(10312188117778823052)
XLA Ops:
  7.9 4.6 %fusion.83 = f32[128,2048]{1,0:T(8,128)S(1)} fusion(bf16[128,2048]{1,0:T(8,128)(2,1)S(1)} %reshape.147, bf16[2048,2048]{1,0:T(8,128)(2,1)} %param.15), kind=kOutput, calls=%fused_computation.102 | convolution fusion | flops 1073741824 | bytes 9961472 | tf_op jit(solution)/shard_map/dot_general | solution.py:54
  15.0 6.7 %copy.91 = bf16[4,2304,256]{1,2,0:T(8,128)(2,1)} copy(bf16[4,2304,256]{2,1,0:T(8,128)(2,1)} %param.20) | data formatting | bytes 9437184 | tf_op args[6]
  21.7 6.6 %copy.99 = bf16[4,2304,2,128]{3,1,2,0:T(8,128)(2,1)} copy(bf16[4,2304,2,128]{1,3,2,0:T(8,128)(2,1)} %bitcast.127) | data formatting | bytes 9437184
  28.3 6.8 %copy.92 = bf16[4,2304,256]{1,2,0:T(8,128)(2,1)} copy(bf16[4,2304,256]{2,1,0:T(8,128)(2,1)} %param.21) | data formatting | bytes 9437184 | tf_op args[7]
  36.5 43.4 %all_gather.6 = bf16[4,128,256]{2,0,1:T(4,128)(2,1)S(1)} all-gather(bf16[4,8,256]{2,0,1:T(4,128)(2,1)S(1)} %copy.93), channel_id=1, replica_groups=mesh['ctx'=16,'head'=2] {'ctx'}, dimensions={1}, use_global_device_ids=true | all-gather | bytes 278528 | tf_op jit(solution)/shard_map/all_gather | solution.py:93
  80.3 20.6 %while.22 = (s32[]{:T(128)}, f32[4,128,256]{2,0,1:T(4,128)S(1)}, bf16[4,2304,2,128]{1,3,2,0:T(8,128)(2,1)}, s32[4,128]{1,0:T(4,128)S(1)}, bf16[4,128,256]{1,2,0:...) while((s32[]{:T(128)}, f32[4,128,256]{2,0,1:T(4,128)S(1)}, ...), condition=%wide.region_3.4_spmd.clone, body=%wide.region_2.3_spmd.clone.sunk | while | flops 306415872 | bytes 3822197 | solution.py:94
  80.6 2.9 fusion.112
  83.6 1.8 dynamic_update_slice.11
  85.8 2.9 fusion.112
  88.8 1.8 dynamic_update_slice.11
  90.9 2.9 fusion.112
  96.0 2.9 fusion.112
  99.0 1.8 dynamic_update_slice.11
  105.3 101.5 %all-reduce.10.cloned.1.call-done = f32[4,128,256]{2,0,1:T(4,128)} async-done(((f32[4,128,256]{2,0,1:T(4,128)}), f32[4,128,256]{2,0,1:T(4,128)}) %all-reduce.10.cloned.1.call-update) | async-done | bytes 524304
  209.1 40.1 %all_gather.7 = bf16[4,128,256]{2,0,1:T(4,128)(2,1)S(1)} all-gather(bf16[4,8,256]{2,0,1:T(4,128)(2,1)S(1)} %fusion.63), channel_id=1, replica_groups=mesh['ctx'=16,'head'=2] {'ctx'}, dimensions={1}, use_global_device_ids=true | all-gather | bytes 278528 | tf_op jit(solution)/shard_map/all_gather | solution.py:97
  250.1 40.3 %while.23 = (s32[]{:T(128)}, f32[4,128,256]{2,0,1:T(4,128)S(1)}, bf16[4,2304,2,128]{3,1,2,0:T(8,128)(2,1)}, s32[4,128]{1,0:T(4,128)S(1)}, bf16[4,128,256]{1,2,0:...) while((s32[]{:T(128)}, f32[4,128,256]{2,0,1:T(4,128)S(1)}, ...), condition=%wide.region_8.9_spmd.clone, body=%wide.region_7.8_spmd.clone.sunk | while | flops 459802880 | bytes 9917057 | solution.py:126
  251.3 3.2 convolution_multiply_fusion.4
  254.5 3.8 fusion.119
  258.4 1.8 dynamic_update_slice.12
  261.3 3.2 convolution_multiply_fusion.4
  264.6 3.8 fusion.119
  268.4 1.8 dynamic_update_slice.12
  271.4 3.2 convolution_multiply_fusion.4
  274.6 3.7 fusion.119
  281.5 3.2 convolution_multiply_fusion.4
  284.7 3.8 fusion.119
  288.6 1.8 dynamic_update_slice.12
  291.4 105.0 %all-reduce.12.cloned.1.call-done = f32[4,128,256]{2,0,1:T(4,128)} async-done(((f32[4,128,256]{2,0,1:T(4,128)}), f32[4,128,256]{2,0,1:T(4,128)}) %all-reduce.12.cloned.1.call-update) | async-done | bytes 524304
  399.4 3.6 psum.15
  405.3 1.9 multiply_convert_fusion
  407.4 7.1 %fusion.48 = bf16[4,8,4,2048]{3,1,2,0:T(8,128)(2,1)} fusion(bf16[2048,2048]{1,0:T(8,128)(2,1)} %param.15, bf16[4,8,4,2048]{3,2,1,0:T(4,128)(2,1)S(1)} %dot_general.52), kind=kOutput, calls=%fused_computation.49 | convolution fusion | flops 1074003968 | bytes 9437184 | tf_op jit(solution)/shard_map/dot_general | solution.py:15
  415.8 16.5 %all-reduce.14.cloned.1.call-done = bf16[4,8,4,2048]{3,1,2,0:T(8,128)(2,1)} async-done(((bf16[4,8,4,2048]{3,1,2,0:T(8,128)(2,1)}), bf16[4,8,4,2048]{3,1,2,0:T(8,128)(2,1)}) %all-reduce.14.cloned.1.call-update) | async-done | bytes 524304
  (106 shorter events, 31.4 us)
Async XLA Ops:
  6.5 7.0 %copy-start = (bf16[2048,512]{1,0:T(8,128)(2,1)S(1)}, bf16[2048,512]{1,0:T(8,128)(2,1)}, u32[]{:S(2)}) copy-start(bf16[2048,512]{1,0:T(8,128)(2,1)} %param.16) | copy-start | bytes 6291460
  6.5 29.0 %all-reduce.8.cloned.1.call-start = ((), (), s32[]{:S(2)}) async-start(), calls=%async_computation | async-start | bytes 131072 | tf_op jit(solution)/shard_map/psum | solution.py:59
  12.5 1.0 copy-start.1
  14.9 191.9 %all-reduce.10.cloned.1.call-start = ((), (), s32[]{:S(2)}) async-start(), calls=%async_computation.1 | async-start | bytes 1048576
  28.3 7.2 %copy-start.4 = (bf16[512,256]{1,0:T(8,128)(2,1)S(1)}, bf16[512,256]{1,0:T(8,128)(2,1)}, u32[]{:S(2)}) copy-start(bf16[512,256]{1,0:T(8,128)(2,1)} %param.17) | copy-start | bytes 786436
  28.3 52.0 %copy-start.6 = (s32[4,128]{1,0:T(4,128)S(1)}, s32[4,128]{1,0:T(4,128)}, u32[]{:S(2)}) copy-start(s32[4,128]{1,0:T(4,128)} %param.22) | copy-start | bytes 6148
  80.3 21.5 %copy-start.5 = (bf16[4,8,512]{2,1,0:T(8,128)(2,1)S(1)}, bf16[4,8,512]{2,1,0:T(8,128)(2,1)}, u32[]{:S(2)}) copy-start(bf16[4,8,512]{2,1,0:T(8,128)(2,1)} %param.23) | copy-start | bytes 98308
  80.3 22.6 %copy-start.8 = (u32[32]{0:T(128)S(1)}, u32[32]{0:T(128)}, u32[]{:S(2)}) copy-start(u32[32]{0:T(128)} %constant.72) | copy-start | bytes 388
  100.9 0.8 copy-start.3
  101.7 294.6 %all-reduce.12.cloned.1.call-start = ((), (), s32[]{:S(2)}) async-start(), calls=%async_computation.2 | async-start | bytes 1048576
  290.4 0.8 copy-start.2
  291.2 141.1 %all-reduce.14.cloned.1.call-start = ((), (), s32[]{:S(2)}) async-start(), calls=%async_computation.3 | async-start | bytes 1048576
  407.4 7.1 %copy-start.7 = (u32[32]{0:T(128)S(1)}, u32[32]{0:T(128)}, u32[]{:S(2)}) copy-start(u32[32]{0:T(128)} %constant.80) | copy-start | bytes 388
Sparse Core Ops, SparseCore 0:
  15.0 20.4 all-reduce.7
  101.8 104.9 all-reduce.9
  291.3 104.9 all-reduce.11
  414.7 17.5 all-reduce.13
where the time goes:
time: 442 us; the launch traced here: 441 us
  waiting for transfers between devices  223 us (50%)
  blocking collectives  87.1 us (20%)
  matrix products  57.8 us (13%)
  local copies, waits for them, and re-layouts  51.4 us (12%)
  between operations  14.7 us (3%)
  other arithmetic  5.77 us (1%)
    unnamed x7, waiting for transfers between devices  223 us
    all_gather x1, blocking collectives, body(): queries_all = lax.all_gather(queries, 'ctx', axis=1, tiled=True)  43.4 us
    all_gather x1, blocking collectives, body(): grads_all = lax.all_gather(attn_grad, 'ctx', axis=1, tiled=True)  40.1 us
    unnamed x29, local copies, waits for them, and re-layouts  27.7 us
    dynamic_update_slice x16, local copies, waits for them, and re-layouts, body(): lax.map(forward_user, (queries_all, cutoffs, key_heads, value_heads))  15.6 us
    dot_general x4, matrix products, backward_user(): jnp.einsum('htp,phd->thd', grad_scores, user_keys, preferred_element_type...  15 us
    dot_general x4, matrix products, backward_user(): jnp.einsum('thd,phd->htp', user_queries.reshape(row_count, heads_here, DH...  12.8 us
    dot_general x4, matrix products, forward_user(): jnp.einsum('htp,phd->thd', weights, user_values, preferred_element_type=j...  11.5 us
  transfers between devices with their start and end apart: 4, of which 4 were waited for; matrix products, arithmetic and copies ran while one was open for 5% of the time, Pallas kernels for 0%

commit v1 on v0

v1 whole, which is shorter than its diff:
```python
import functools

import jax
import jax.numpy as jnp
from jax import lax
from jax.experimental import pallas as pl
from jax.experimental.pallas import tpu as pltpu
from jax.sharding import PartitionSpec as P

DH = 128
F32 = jnp.float32
BF16 = jnp.bfloat16


def matmul(left, right):
    return jnp.dot(left, right, preferred_element_type=F32)


def contract_last(left, right):
    return lax.dot_general(left, right, (((1,), (1,)), ((), ())), preferred_element_type=F32)


def silu_parts(half):
    tanh = jnp.tanh(half)
    value = half + half * tanh
    slope = 0.5 * (1.0 + tanh) * (1.0 + half * (1.0 - tanh))
    return value, slope


def whole(shape):
    return pl.BlockSpec(shape, lambda *_: (0,) * len(shape))


def params(*semantics):
    return pltpu.CompilerParams(dimension_semantics=semantics, vmem_limit_bytes=40 << 20)


def encode_kernel(parts, rows_ref, wh_ref, we_ref, slope_ref, out_ref, acc_ref):
    step = pl.program_id(0)
    lin = matmul(rows_ref[...], wh_ref[...])
    value, slope = silu_parts(0.5 * lin)
    slope_ref[...] = slope
    part = matmul(value.astype(BF16), we_ref[...])

    @pl.when(step == 0)
    def _():
        acc_ref[...] = part

    @pl.when(step > 0)
    def _():
        acc_ref[...] += part

    @pl.when(step == pl.num_programs(0) - 1)
    def _():
        count = out_ref.shape[0]
        total = acc_ref[0:count]
        for part_index in range(1, parts):
            total = total + acc_ref[part_index * count : (part_index + 1) * count]
        out_ref[...] = total


def encode(rows, w_hidden, w_embed, parts, block):
    count, width = rows.shape
    hidden = w_hidden.shape[1]
    model = w_embed.shape[1]
    return pl.pallas_call(
        functools.partial(encode_kernel, parts),
        grid=(hidden // block,),
        in_specs=[
            whole(rows.shape),
            pl.BlockSpec((width, block), lambda j: (0, j)),
            pl.BlockSpec((block, model), lambda j: (j, 0)),
        ],
        out_specs=[
            pl.BlockSpec((count, block), lambda j: (0, j)),
            whole((count // parts, model)),
        ],
        out_shape=[
            jax.ShapeDtypeStruct((count, hidden), F32),
            jax.ShapeDtypeStruct((count // parts, model), F32),
        ],
        scratch_shapes=[pltpu.VMEM((count, model), F32)],
        compiler_params=params("arbitrary"),
        name="encode",
    )(rows, w_hidden, w_embed)


def project_kernel(
    mine_ref, other_ref, wq_ref, wg_ref, wp_ref, cot_ref, send_ref, gates_ref, og_ref, qs_ref, gs_ref
):
    embedded = (0.5 * (mine_ref[...] + other_ref[...])).astype(BF16)
    query, query_slope = silu_parts(0.5 * matmul(embedded, wq_ref[...]))
    gate, gate_slope = silu_parts(0.5 * matmul(embedded, wg_ref[...]))
    qs_ref[...] = query_slope
    gs_ref[...] = gate_slope
    gates_ref[...] = gate.astype(BF16).astype(F32)
    og_ref[...] = contract_last(cot_ref[...], wp_ref[...]).astype(BF16).astype(F32)
    block = query.reshape(send_ref.shape[1:]).astype(BF16)
    for index in range(send_ref.shape[0]):
        send_ref[index] = block


def project(mine, other, w_query, w_gate, w_proj, cotangent, copies, users):
    count = mine.shape[0]
    local = w_query.shape[1]
    rows = jax.ShapeDtypeStruct((count, local), F32)
    return pl.pallas_call(
        project_kernel,
        out_shape=[jax.ShapeDtypeStruct((copies, users, count // users, local), BF16)] + [rows] * 4,
        compiler_params=params(),
        name="project",
    )(mine, other, w_query, w_gate, w_proj, cotangent)


def forward_kernel(scale, heads, query_ref, limit_ref, key_ref, value_ref, out_ref, slope_ref, q_ref, acc_ref):
    step = pl.program_id(1)

    @pl.when(step == 0)
    def _():
        q_ref[...] = query_ref[...].astype(F32).reshape(q_ref.shape).astype(BF16)
        acc_ref[...] = jnp.zeros_like(acc_ref)

    targets, events = q_ref.shape[0], key_ref.shape[1]
    spots = lax.broadcasted_iota(jnp.int32, (targets, events), 1) + step * events
    visible = spots < limit_ref[0]
    for head in range(heads):
        lanes = slice(head * DH, (head + 1) * DH)
        half = contract_last(q_ref[:, lanes], key_ref[0, :, lanes]) * (0.5 * scale)
        value, slope = silu_parts(half)
        weights = jnp.where(visible, value, 0.0).astype(BF16)
        slope_ref[0, head] = jnp.where(visible, slope, 0.0).astype(BF16)
        acc_ref[:, lanes] += matmul(weights, value_ref[0, :, lanes])

    @pl.when(step == pl.num_programs(1) - 1)
    def _():
        out_ref[...] = acc_ref[...].reshape(out_ref.shape).astype(BF16)


def forward_attention(queries, limits, keys, values, heads, block):
    copies, users, rows, local = queries.shape
    events = keys.shape[1]
    targets = copies * rows
    spread = pl.BlockSpec((copies, 1, rows, local), lambda u, e: (0, u, 0, 0))
    event_block = pl.BlockSpec((1, block, local), lambda u, e: (u, e, 0))
    return pl.pallas_call(
        functools.partial(forward_kernel, DH ** (-0.5), heads),
        grid=(users, events // block),
        in_specs=[
            spread,
            pl.BlockSpec((1, targets, 1), lambda u, e: (u, 0, 0)),
            event_block,
            event_block,
        ],
        out_specs=[
            spread,
            pl.BlockSpec((1, heads, targets, block), lambda u, e: (u, 0, 0, e)),
        ],
        out_shape=[
            jax.ShapeDtypeStruct(queries.shape, BF16),
            jax.ShapeDtypeStruct((users, heads, targets, events), BF16),
        ],
        scratch_shapes=[
            pltpu.VMEM((targets, local), BF16),
            pltpu.VMEM((targets, local), F32),
        ],
        compiler_params=params("arbitrary", "arbitrary"),
        name="attention_forward",
    )(queries, limits, keys, values)


def norm_kernel(heads, parts_ref, gates_ref, og_ref, send_ref, gg_ref):
    total = parts_ref[0].astype(F32)
    for index in range(1, parts_ref.shape[0]):
        total = total + parts_ref[index].astype(F32)
    attended = total.reshape(gates_ref.shape)
    pieces = []
    for head in range(heads):
        lanes = slice(head * DH, (head + 1) * DH)
        rows = attended[:, lanes]
        rscale = lax.rsqrt(jnp.mean(rows * rows, axis=-1, keepdims=True) + 1e-06)
        normed = rows * rscale
        out_grad = og_ref[:, lanes]
        gg_ref[:, lanes] = out_grad * normed
        normed_grad = out_grad * gates_ref[:, lanes]
        mean = jnp.mean(normed_grad * normed, axis=-1, keepdims=True)
        pieces.append(rscale * (normed_grad - normed * mean))
    grad = jnp.concatenate(pieces, axis=-1)
    block = grad.reshape(send_ref.shape[1:]).astype(BF16)
    for index in range(send_ref.shape[0]):
        send_ref[index] = block


def norm_grads(partials, gates, out_grad, heads):
    return pl.pallas_call(
        functools.partial(norm_kernel, heads),
        out_shape=[
            jax.ShapeDtypeStruct(partials.shape, BF16),
            jax.ShapeDtypeStruct(gates.shape, F32),
        ],
        compiler_params=params(),
        name="norm_grads",
    )(partials, gates, out_grad)


def backward_kernel(scale, heads, grad_ref, slope_ref, key_ref, value_ref, out_ref, g_ref, acc_ref):
    step = pl.program_id(1)

    @pl.when(step == 0)
    def _():
        g_ref[...] = grad_ref[...].astype(F32).reshape(g_ref.shape).astype(BF16)
        acc_ref[...] = jnp.zeros_like(acc_ref)

    for head in range(heads):
        lanes = slice(head * DH, (head + 1) * DH)
        weight_grad = contract_last(g_ref[:, lanes], value_ref[0, :, lanes])
        grad_scores = (weight_grad * slope_ref[0, head].astype(F32)).astype(BF16)
        acc_ref[:, lanes] += matmul(grad_scores, key_ref[0, :, lanes])

    @pl.when(step == pl.num_programs(1) - 1)
    def _():
        out_ref[...] = (acc_ref[...] * scale).reshape(out_ref.shape).astype(BF16)


def backward_attention(grads, slopes, keys, values, heads, block):
    copies, users, rows, local = grads.shape
    events = keys.shape[1]
    targets = copies * rows
    spread = pl.BlockSpec((copies, 1, rows, local), lambda u, e: (0, u, 0, 0))
    event_block = pl.BlockSpec((1, block, local), lambda u, e: (u, e, 0))
    return pl.pallas_call(
        functools.partial(backward_kernel, DH ** (-0.5), heads),
        grid=(users, events // block),
        in_specs=[
            spread,
            pl.BlockSpec((1, heads, targets, block), lambda u, e: (u, 0, 0, e)),
            event_block,
            event_block,
        ],
        out_specs=spread,
        out_shape=jax.ShapeDtypeStruct(grads.shape, BF16),
        scratch_shapes=[
            pltpu.VMEM((targets, local), BF16),
            pltpu.VMEM((targets, local), F32),
        ],
        compiler_params=params("arbitrary", "arbitrary"),
        name="attention_backward",
    )(grads, slopes, keys, values)


def embed_kernel(parts_ref, gg_ref, qs_ref, gs_ref, wq_ref, wg_ref, out_ref):
    total = parts_ref[0].astype(F32)
    for index in range(1, parts_ref.shape[0]):
        total = total + parts_ref[index].astype(F32)
    query_back = (total.reshape(qs_ref.shape) * qs_ref[...]).astype(BF16)
    gate_back = (gg_ref[...] * gs_ref[...]).astype(BF16)
    out_ref[...] = contract_last(query_back, wq_ref[...]) + contract_last(gate_back, wg_ref[...])


def embed_grads(partials, gate_grad, query_slope, gate_slope, w_query, w_gate):
    return pl.pallas_call(
        embed_kernel,
        out_shape=jax.ShapeDtypeStruct((gate_grad.shape[0], w_query.shape[0]), F32),
        compiler_params=params(),
        name="embed_grads",
    )(partials, gate_grad, query_slope, gate_slope, w_query, w_gate)


def content_kernel(parts, mine_ref, other_ref, we_ref, slope_ref, wh_ref, head_ref, keep_ref, send_ref, back_ref):
    count = mine_ref.shape[0]
    half = back_ref.shape[0] // 2

    @pl.when(pl.program_id(0) == 0)
    def _():
        embed_grad = (0.5 * (mine_ref[...] + other_ref[...])).astype(BF16)
        hidden_grad = contract_last(embed_grad, we_ref[...])
        for index in range(parts):
            rows = slice(index * count, (index + 1) * count)
            back_ref[rows] = (hidden_grad * slope_ref[rows]).astype(BF16)

    head = head_ref[0]
    kept = pl.multiple_of(head * half, half)
    sent = pl.multiple_of((1 - head) * half, half)
    keep_ref[...] = contract_last(back_ref[pl.ds(kept, half), :], wh_ref[...])
    send_ref[...] = contract_last(back_ref[pl.ds(sent, half), :], wh_ref[...]).astype(BF16)


def content_grads(mine, other, w_embed, slopes, w_hidden, head, parts, block):
    count, hidden = slopes.shape
    width = w_hidden.shape[0]
    columns = pl.BlockSpec((count // 2, block), lambda j: (0, j))
    return pl.pallas_call(
        functools.partial(content_kernel, parts),
        grid=(width // block,),
        in_specs=[
            whole(mine.shape),
            whole(other.shape),
            whole(w_embed.shape),
            whole(slopes.shape),
            pl.BlockSpec((block, hidden), lambda j: (j, 0)),
            pl.BlockSpec(memory_space=pltpu.SMEM),
        ],
        out_specs=[columns, columns],
        out_shape=[
            jax.ShapeDtypeStruct((count // 2, width), F32),
            jax.ShapeDtypeStruct((count // 2, width), BF16),
        ],
        scratch_shapes=[pltpu.VMEM((count, hidden), BF16)],
        compiler_params=params("arbitrary"),
        name="content_grads",
    )(mine, other, w_embed, slopes, w_hidden, head)


def body(
    head_count,
    content_rows,
    w_hidden,
    w_embed,
    w_query,
    w_gate,
    w_proj,
    history_keys,
    history_values,
    cutoffs,
    out_cotangent,
):
    users, shard_rows, parts, width = content_rows.shape
    local = w_query.shape[1]
    heads = local // DH
    events = history_keys.shape[1]
    count = users * shard_rows
    copies = cutoffs.shape[1] // shard_rows
    swap = [(index, (index + 1) % head_count) for index in range(head_count)]
    head = lax.axis_index("head").astype(jnp.int32)

    def to_owner(blocks):
        return lax.all_to_all(blocks, "ctx", 0, 0, tiled=True)

    rows = content_rows.reshape(count, parts, width).transpose(1, 0, 2).reshape(-1, width)
    hidden_slope, mine = encode(rows, w_hidden, w_embed, parts, 512)
    other = lax.ppermute(mine, "head", swap)
    cotangent = out_cotangent.reshape(count, -1)
    sends, gates, out_grad, query_slope, gate_slope = project(
        mine, other, w_query, w_gate, w_proj, cotangent, copies, users
    )
    queries = to_owner(sends)
    limits = (cutoffs - lax.axis_index("ctx") * events)[:, :, None]
    block = events // 3
    partial, slopes = forward_attention(queries, limits, history_keys, history_values, heads, block)
    sends, gate_grad = norm_grads(to_owner(partial), gates, out_grad, heads)
    grads = to_owner(sends)
    partial = backward_attention(grads, slopes, history_keys, history_values, heads, block)
    mine = embed_grads(to_owner(partial), gate_grad, query_slope, gate_slope, w_query, w_gate)
    other = lax.ppermute(mine, "head", swap)
    keep, send = content_grads(
        mine, other, w_embed, hidden_slope, w_hidden, head[None], parts, 512
    )
    got = lax.ppermute(send, "head", swap)
    total = (keep + got.astype(F32)).astype(BF16)
    half = parts // head_count
    return total.reshape(half, count, width).transpose(1, 0, 2).reshape(users, shard_rows, half, width)


def solution(mesh):
    in_specs = (
        P(None, "ctx", None, None),
        P(None, "head"),
        P("head", None),
        P(None, "head"),
        P(None, "head"),
        P("head", None),
        P(None, "ctx", "head"),
        P(None, "ctx", "head"),
        P(),
        P(None, "ctx", None),
    )
    out_specs = P(None, "ctx", "head", None)
    return jax.shard_map(
        functools.partial(body, mesh.shape["head"]),
        mesh=mesh,
        in_specs=in_specs,
        out_specs=out_specs,
        check_vma=False,
    )
```

time: 442 us -> 109 us (0.25)
  waiting for transfers between devices: 223 us -> 13.5 us
  matrix products: 57.8 us -> 0 us
  blocking collectives: 87.1 us -> 37.9 us
  local copies, waits for them, and re-layouts: 51.4 us -> 13.2 us
  Pallas kernels: 0 us -> 33.9 us
  between operations: 14.7 us -> 0.13 us
  starting transfers between devices: 0.13 us -> 8.99 us
  other arithmetic: 5.77 us -> 0.07 us
    unnamed x7 -> x0, waiting for transfers between devices: 223 us -> none
    all_gather x2 -> x0, blocking collectives: 83.5 us -> none  [the longest x1 43.4 us: body(): queries_all = lax.all_gather(queries, 'ctx', axis=1, tiled=True)]
    dot_general x21 -> x0, matrix products: 57.8 us -> none  [the longest x4 15 us: backward_user(): jnp.einsum('htp,phd->thd', grad_scores, user_keys, preferred_element_type...]
    all_to_all x0 -> x3, blocking collectives: none -> 37.9 us  [to_owner(): return lax.all_to_all(blocks, 'ctx', 0, 0, tiled=True)]
    pallas_call x0 -> x7, Pallas kernels: none -> 33.9 us  [the longest x1 12.1 us: forward_attention(): pl.pallas_call(functools.partial(forward_kernel, DH ** (-0.5), heads), gr...]
    unnamed x29 -> x24, local copies, waits for them, and re-layouts: 27.7 us -> 10.7 us
    dynamic_update_slice x16 -> x0, local copies, waits for them, and re-layouts: 15.6 us -> none  [body(): lax.map(forward_user, (queries_all, cutoffs, key_heads, value_heads))]
    all_to_all x0 -> x1, waiting for transfers between devices: none -> 10 us  [to_owner(): return lax.all_to_all(blocks, 'ctx', 0, 0, tiled=True)]
  transfers between devices with their start and end apart: 4 -> 4, of which waited for: 4 -> 4; matrix products, arithmetic and copies ran while one was open for 5% -> 0% of each run, Pallas kernels for 0% -> 0%
where the time goes in v1:
time: 109 us; the launch traced here: 108 us
  blocking collectives  37.9 us (35%)
  Pallas kernels  33.9 us (31%)
  waiting for transfers between devices  13.5 us (12%)
  local copies, waits for them, and re-layouts  13.2 us (12%)
  starting transfers between devices  8.99 us (8%)
    all_to_all x3, blocking collectives, to_owner(): return lax.all_to_all(blocks, 'ctx', 0, 0, tiled=True)  37.9 us
    pallas_call x1, Pallas kernels, forward_attention(): pl.pallas_call(functools.partial(forward_kernel, DH ** (-0.5), heads), gr...  12.1 us
    unnamed x24, local copies, waits for them, and re-layouts  10.7 us
    pallas_call x1, Pallas kernels, backward_attention(): pl.pallas_call(functools.partial(backward_kernel, DH ** (-0.5), heads), g...  10.4 us
    all_to_all x1, waiting for transfers between devices, to_owner(): return lax.all_to_all(blocks, 'ctx', 0, 0, tiled=True)  10 us
    all_to_all x1, starting transfers between devices, to_owner(): return lax.all_to_all(blocks, 'ctx', 0, 0, tiled=True)  8.21 us
    pallas_call x1, Pallas kernels, content_grads(): pl.pallas_call(functools.partial(content_kernel, parts), grid=(width // b...  6.33 us
    pallas_call x1, Pallas kernels, encode(): pl.pallas_call(functools.partial(encode_kernel, parts), grid=(hidden // b...  3.64 us
  transfers between devices with their start and end apart: 4, of which 4 were waited for; matrix products, arithmetic and copies ran while one was open for 0% of the time, Pallas kernels for 0%

profile of v1, /device:TPU:0, one launch (start us, length us, event | category | flops | bytes accessed | tf_op | source)
XLA Modules:
  0.0 107.8 jit_solution(14484417319860389895)
XLA Ops:
  0.0 1.3 %copy.13 = bf16[32,4,2048]{2,0,1:T(8,128)(2,1)S(1)} copy(bf16[32,4,2048]{2,1,0:T(4,128)(2,1)} %bitcast.15) | data formatting | bytes 1048576 | tf_op jit(solution)/shard_map/reshape | solution.py:338
  1.3 0.0 copy-start
  1.3 3.4 %copy-done = bf16[2048,2048]{1,0:T(8,128)(2,1)S(1)} copy-done((bf16[2048,2048]{1,0:T(8,128)(2,1)S(1)}, bf16[2048,2048]{1,0:T(8,128)(2,1)}, u32[]{:S(2)}) %copy-start) | copy-done | bytes 8388632
  4.7 1.6 %copy-done.4 = bf16[2048,512]{1,0:T(8,128)(2,1)S(1)} copy-done((bf16[2048,512]{1,0:T(8,128)(2,1)S(1)}, bf16[2048,512]{1,0:T(8,128)(2,1)}, u32[]{:S(2)}) %copy-start.4) | copy-done | bytes 2097176
  6.3 0.0 copy-start.11
  6.3 3.6 %encode.1 = (f32[128,2048]{1,0:T(8,128)S(1)}, f32[32,512]{1,0:T(8,128)S(1)}) custom-call(bf16[128,2048]{1,0:T(8,128)(2,1)S(1)} %bitcast.12, bf16[2048,2048]{1,0:T(8,128)(2,1)S(1)} %copy-done, bf16[2048,512]{1,0:T(8,128)(2,1)S(1)} %copy-done.4), custom_call_target="tpu_custom_call" | custom-call | tf_op jit(solution)/shard_map/encode/pallas_call | solution.py:66
  10.0 0.6 collective-permute-start
  10.5 0.9 collective-permute-done.other_ref
  11.4 0.0 copy-done.6
  11.4 0.0 copy-done.7
  11.5 0.0 copy-done.10
  11.5 0.9 project.1
  12.4 8.2 %all-to-all-start = ((bf16[16,4,8,256]{3,2,1,0:T(8,128)(2,1)}), bf16[16,4,8,256]{3,2,1,0:T(8,128)(2,1)S(1)}, u32[]{:S(2)}, u32[]{:S(2)}) async-start(bf16[16,4,8,256]{3,2,1,0:T(8,128)(2,1)} %get-tuple-element.19), calls=%async_computation | async-start | bytes 524288 | tf_op jit(solution)/shard_map/all_to_all | solution.py:336
  20.6 0.1 copy.14.limit_ref
  20.8 10.0 %all-to-all-done.query_ref = bf16[16,4,8,256]{3,2,1,0:T(8,128)(2,1)S(1)} async-done(((bf16[16,4,8,256]{3,2,1,0:T(8,128)(2,1)}), bf16[16,4,8,256]{3,2,1,0:T(8,128)(2,1)S(1)}, u32[]{:S(2)}, u32[]{:S(2)}) %all-to-all-start) | async-done | bytes 262176 | tf_op jit(solution)/shard_map/all_to_all | solution.py:336
  30.8 2.3 %copy-done.2 = bf16[4,2304,256]{2,1,0:T(8,128)(2,1)S(1)} copy-done((bf16[4,2304,256]{2,1,0:T(8,128)(2,1)S(1)}, bf16[4,2304,256]{2,1,0:T(8,128)(2,1)}, u32[]{:S(2)}) %copy-start.2) | copy-done | bytes 4718616
  33.1 12.1 %attention_forward.1 = (bf16[16,4,8,256]{3,2,1,0:T(8,128)(2,1)S(1)}, bf16[4,2,128,2304]{3,2,1,0:T(8,128)(2,1)S(1)}) custom-call(bf16[16,4,8,256]{3,2,1,0:T(8,128)(2,1)S(1)} %all-to-all-done.query_ref, s32[4,128,1]{2,1,0:T(8,128)S(1)} %copy.14.limit_ref, bf16[4,2304,256]{2,1,0:T(8,128)(2,1)S(1)} %copy-done.2, bf16[4,2304,256]{2,1,0:T(8,128)(2,1)} %value_ref.3), custom_call_target="tpu_custom_call" | custom-call | tf_op jit(solution)/shard_map/attention_forward/pallas_call | solution.py:145
  45.3 12.8 %all_to_all.20.parts_ref = bf16[16,4,8,256]{3,2,1,0:T(8,128)(2,1)S(1)} all-to-all(bf16[16,4,8,256]{3,2,1,0:T(8,128)(2,1)S(1)} %get-tuple-element.20), channel_id=1, replica_groups=mesh['ctx'=16,'head'=2] {'ctx'}, dimensions={0} | all-to-all | bytes 524288 | tf_op jit(solution)/shard_map/all_to_all | solution.py:336
  58.1 0.2 norm_grads.1
  58.3 12.6 %all_to_all.21.grad_ref = bf16[16,4,8,256]{3,2,1,0:T(8,128)(2,1)S(1)} all-to-all(bf16[16,4,8,256]{3,2,1,0:T(8,128)(2,1)S(1)} %get-tuple-element.23), channel_id=1, replica_groups=mesh['ctx'=16,'head'=2] {'ctx'}, dimensions={0} | all-to-all | bytes 524288 | tf_op jit(solution)/shard_map/all_to_all | solution.py:336
  70.9 0.0 copy-done.3
  70.9 10.4 %attention_backward.1 = bf16[16,4,8,256]{3,2,1,0:T(8,128)(2,1)S(1)} custom-call(bf16[16,4,8,256]{3,2,1,0:T(8,128)(2,1)S(1)} %all_to_all.21.grad_ref, bf16[4,2,128,2304]{3,2,1,0:T(8,128)(2,1)S(1)} %get-tuple-element.24.slope_ref, bf16[4,2304,256]{2,1,0:T(8,128)(2,1)S(1)} %copy-done.3, bf16[4,2304,256]{2,1,0:T(8,128)(2,1)} %value_ref.3), custom_call_target="tpu_custom_call" | custom-call | tf_op jit(solution)/shard_map/attention_backward/pallas_call | solution.py:230
  81.4 12.5 %all_to_all.22.parts_ref = bf16[16,4,8,256]{3,2,1,0:T(8,128)(2,1)S(1)} all-to-all(bf16[16,4,8,256]{3,2,1,0:T(8,128)(2,1)S(1)} %attention_backward.1), channel_id=1, replica_groups=mesh['ctx'=16,'head'=2] {'ctx'}, dimensions={0} | all-to-all | bytes 524288 | tf_op jit(solution)/shard_map/all_to_all | solution.py:336
  93.9 0.2 embed_grads.1.mine_ref
  94.2 0.0 collective-permute-start.1
  94.2 1.3 %collective-permute-done.1.other_ref = f32[32,512]{1,0:T(8,128)S(1)} collective-permute-done((f32[32,512]{1,0:T(8,128)S(1)}, f32[32,512]{1,0:T(8,128)S(1)}, u32[]{:S(2)}, u32[]{:S(2)}) %collective-permute-start.1) | collective-permute-done | bytes 65568 | tf_op jit(solution)/shard_map/ppermute | solution.py:353
  95.4 3.4 %copy-done.1 = bf16[2048,2048]{1,0:T(8,128)(2,1)S(1)} copy-done((bf16[2048,2048]{1,0:T(8,128)(2,1)S(1)}, bf16[2048,2048]{1,0:T(8,128)(2,1)}, u32[]{:S(2)}) %copy-start.1) | copy-done | bytes 8388632
  98.8 6.3 %content_grads.1 = (f32[64,2048]{1,0:T(8,128)S(1)}, bf16[64,2048]{1,0:T(8,128)(2,1)S(1)}) custom-call(f32[32,512]{1,0:T(8,128)S(1)} %embed_grads.1.mine_ref, f32[32,512]{1,0:T(8,128)S(1)} %collective-permute-done.1.other_ref, bf16[2048,512]{1,0:T(8,128)(2,1)S(1)} %copy-done.5, f32[128,2048]{1,0:T(8,128)S(1)} %get-tuple-element.28.slope_ref, ...), custom_call_target="tpu_custom_call" | custom-call | tf_op jit(solution)/shard_map/content_grads/pallas_call | solution.py:291
  105.2 0.2 collective-permute-start.2
  105.4 1.4 %collective-permute-done.2 = bf16[64,2048]{1,0:T(8,128)(2,1)S(1)} collective-permute-done((bf16[64,2048]{1,0:T(8,128)(2,1)S(1)}, bf16[64,2048]{1,0:T(8,128)(2,1)S(1)}, u32[]{:S(2)}, u32[]{:S(2)}) %collective-permute-start.2) | collective-permute-done | bytes 262176 | tf_op jit(solution)/shard_map/ppermute | solution.py:357
  106.8 0.1 add_convert_fusion
  106.8 1.0 copy.15
  (15 shorter events, 0.0 us)
Async XLA Ops:
  1.3 3.4 %copy-start = (bf16[2048,2048]{1,0:T(8,128)(2,1)S(1)}, bf16[2048,2048]{1,0:T(8,128)(2,1)}, u32[]{:S(2)}) copy-start(bf16[2048,2048]{1,0:T(8,128)(2,1)} %wh_ref.3) | copy-start | bytes 25165828
  4.7 1.6 %copy-start.4 = (bf16[2048,512]{1,0:T(8,128)(2,1)S(1)}, bf16[2048,512]{1,0:T(8,128)(2,1)}, u32[]{:S(2)}) copy-start(bf16[2048,512]{1,0:T(8,128)(2,1)} %we_ref.3) | copy-start | bytes 6291460
  6.3 5.1 %copy-start.6 = (bf16[512,256]{1,0:T(8,128)(2,1)S(1)}, bf16[512,256]{1,0:T(8,128)(2,1)}, u32[]{:S(2)}) copy-start(bf16[512,256]{1,0:T(8,128)(2,1)} %wq_ref.3) | copy-start | bytes 786436
  6.3 5.1 %copy-start.7 = (bf16[512,256]{1,0:T(8,128)(2,1)S(1)}, bf16[512,256]{1,0:T(8,128)(2,1)}, u32[]{:S(2)}) copy-start(bf16[512,256]{1,0:T(8,128)(2,1)} %wg_ref.3) | copy-start | bytes 786436
  6.3 5.1 %copy-start.9 = (bf16[256,512]{1,0:T(8,128)(2,1)S(1)}, bf16[256,512]{1,0:T(8,128)(2,1)}, u32[]{:S(2)}) copy-start(bf16[256,512]{1,0:T(8,128)(2,1)} %wp_ref.1) | copy-start | bytes 786436
  6.3 5.1 %copy-start.10 = (bf16[4,8,512]{2,1,0:T(8,128)(2,1)S(1)}, bf16[4,8,512]{2,1,0:T(8,128)(2,1)}, u32[]{:S(2)}) copy-start(bf16[4,8,512]{2,1,0:T(8,128)(2,1)} %param.19) | copy-start | bytes 98308
  6.3 14.3 %copy-start.11 = (s32[4,128]{1,0:T(4,128)S(1)}, s32[4,128]{1,0:T(4,128)}, u32[]{:S(2)}) copy-start(s32[4,128]{1,0:T(4,128)} %param.18) | copy-start | bytes 6148
  10.0 1.5 %collective-permute-start = (f32[32,512]{1,0:T(8,128)S(1)}, f32[32,512]{1,0:T(8,128)S(1)}, u32[]{:S(2)}, u32[]{:S(2)}) collective-permute-start(f32[32,512]{1,0:T(8,128)S(1)} %get-tuple-element.18.mine_ref), channel_id=1, source_target_pairs={{0,1},{1,0},{2,3},{3,2},{4,5},{5,4},{6,7},{7,6},{8,9},{9,8},{10,11... | collective-permute-start | bytes 196616 | tf_op jit(solution)/shard_map/ppermute | solution.py:340
  12.4 18.4 %all-to-all-start = ((bf16[16,4,8,256]{3,2,1,0:T(8,128)(2,1)}), bf16[16,4,8,256]{3,2,1,0:T(8,128)(2,1)S(1)}, u32[]{:S(2)}, u32[]{:S(2)}) async-start(bf16[16,4,8,256]{3,2,1,0:T(8,128)(2,1)} %get-tuple-element.19), calls=%async_computation | async-start | bytes 524288 | tf_op jit(solution)/shard_map/all_to_all | solution.py:336
  30.8 2.3 %copy-start.2 = (bf16[4,2304,256]{2,1,0:T(8,128)(2,1)S(1)}, bf16[4,2304,256]{2,1,0:T(8,128)(2,1)}, u32[]{:S(2)}) copy-start(bf16[4,2304,256]{2,1,0:T(8,128)(2,1)} %key_ref.3) | copy-start | bytes 14155780
  33.1 37.8 %copy-start.3 = (bf16[4,2304,256]{2,1,0:T(8,128)(2,1)S(1)}, bf16[4,2304,256]{2,1,0:T(8,128)(2,1)}, u32[]{:S(2)}) copy-start(bf16[4,2304,256]{2,1,0:T(8,128)(2,1)} %key_ref.3) | copy-start | bytes 14155780
  70.9 23.0 %copy-start.8 = (bf16[512,256]{1,0:T(8,128)(2,1)S(1)}, bf16[512,256]{1,0:T(8,128)(2,1)}, u32[]{:S(2)}) copy-start(bf16[512,256]{1,0:T(8,128)(2,1)} %wg_ref.3) | copy-start | bytes 786436
  70.9 24.5 %copy-start.5 = (bf16[2048,512]{1,0:T(8,128)(2,1)S(1)}, bf16[2048,512]{1,0:T(8,128)(2,1)}, u32[]{:S(2)}) copy-start(bf16[2048,512]{1,0:T(8,128)(2,1)} %we_ref.3) | copy-start | bytes 6291460
  94.2 1.3 %collective-permute-start.1 = (f32[32,512]{1,0:T(8,128)S(1)}, f32[32,512]{1,0:T(8,128)S(1)}, u32[]{:S(2)}, u32[]{:S(2)}) collective-permute-start(f32[32,512]{1,0:T(8,128)S(1)} %embed_grads.1.mine_ref), channel_id=1, source_target_pairs={{0,1},{1,0},{2,3},{3,2},{4,5},{5,4},{6,7},{7,6},{8,9},{9,8},{10,11... | collective-permute-start | bytes 196616 | tf_op jit(solution)/shard_map/ppermute | solution.py:353
  95.4 3.4 %copy-start.1 = (bf16[2048,2048]{1,0:T(8,128)(2,1)S(1)}, bf16[2048,2048]{1,0:T(8,128)(2,1)}, u32[]{:S(2)}) copy-start(bf16[2048,2048]{1,0:T(8,128)(2,1)} %wh_ref.3) | copy-start | bytes 25165828
  105.2 1.6 %collective-permute-start.2 = (bf16[64,2048]{1,0:T(8,128)(2,1)S(1)}, bf16[64,2048]{1,0:T(8,128)(2,1)S(1)}, u32[]{:S(2)}, u32[]{:S(2)}) collective-permute-start(bf16[64,2048]{1,0:T(8,128)(2,1)S(1)} %get-tuple-element.30), channel_id=1, source_target_pairs={{0,1},{1,0},{2,3},{3,2},{4,5},{5,4},{6,7},{7,6},{8,9},{9,8},{10,11... | collective-permute-start | bytes 786440 | tf_op jit(solution)/shard_map/ppermute | solution.py:357

commit v2 on v1

v2 whole, which is shorter than its diff:
```python
import functools

import jax
import jax.numpy as jnp
from jax import lax
from jax.experimental import pallas as pl
from jax.experimental.pallas import tpu as pltpu
from jax.sharding import PartitionSpec as P

DH = 128
F32 = jnp.float32
BF16 = jnp.bfloat16


def matmul(left, right):
    return jnp.dot(left, right, preferred_element_type=F32)


def contract_last(left, right):
    return lax.dot_general(left, right, (((1,), (1,)), ((), ())), preferred_element_type=F32)


def silu_parts(half):
    tanh = jnp.tanh(half)
    lift = 1.0 + tanh
    value = half * lift
    return value, lift + value * (1.0 - tanh)


def params(mebibytes):
    return pltpu.CompilerParams(vmem_limit_bytes=mebibytes << 20)


def in_vmem(count):
    return [pl.BlockSpec(memory_space=pltpu.VMEM)] * count


def in_hbm(array):
    return pltpu.with_memory_space_constraint(array, pltpu.HBM)


def kept_in_vmem(array):
    return pltpu.with_memory_space_constraint(array, pltpu.VMEM)


def chunk_of(length, wanted):
    while length % wanted:
        wanted //= 2
    return wanted


def encode_kernel(parts, block, rows_ref, wh_hbm, we_hbm, slope_ref, out_ref, wh_ref, we_ref, rm_ref, sems):
    total_rows, hidden = slope_ref.shape
    blocks = hidden // block
    count = total_rows // parts
    copies = []
    for index in range(blocks):
        columns = pl.ds(index * block, block)
        copies.append(
            (
                pltpu.make_async_copy(wh_hbm.at[:, columns], wh_ref.at[:, columns], sems.at[0, index]),
                pltpu.make_async_copy(we_hbm.at[columns, :], we_ref.at[columns, :], sems.at[1, index]),
            )
        )
    for pair in copies:
        pair[0].start()
        pair[1].start()
    spot = lax.broadcasted_iota(jnp.int32, (total_rows, total_rows), 0)
    from_row = lax.broadcasted_iota(jnp.int32, (total_rows, total_rows), 1)
    wanted = (spot % count) * parts + spot // count
    order = jnp.where(from_row == wanted, 1.0, 0.0).astype(BF16)
    rows = rows_ref[...].astype(F32).reshape(total_rows, rows_ref.shape[2]).astype(BF16)
    rm_ref[...] = matmul(order, rows).astype(BF16)
    total = jnp.zeros((total_rows, we_ref.shape[1]), F32)
    for index in range(blocks):
        columns = slice(index * block, (index + 1) * block)
        copies[index][0].wait()
        lin = matmul(rm_ref[...], wh_ref[:, columns])
        value, slope = silu_parts(0.5 * lin)
        slope_ref[:, columns] = slope
        copies[index][1].wait()
        total = total + matmul(value.astype(BF16), we_ref[columns, :])
    summed = total[0:count]
    for part in range(1, parts):
        summed = summed + total[part * count : (part + 1) * count]
    out_ref[...] = summed


def encode(content, w_hidden, w_embed, block):
    count, parts, width = content.shape
    hidden = w_hidden.shape[1]
    model = w_embed.shape[1]
    return pl.pallas_call(
        functools.partial(encode_kernel, parts, block),
        in_specs=in_vmem(1) + [pl.BlockSpec(memory_space=pltpu.HBM)] * 2,
        out_specs=in_vmem(4),
        out_shape=[
            pltpu.VMEM((count * parts, hidden), F32),
            jax.ShapeDtypeStruct((count, model), F32),
            pltpu.VMEM(w_hidden.shape, BF16),
            pltpu.VMEM(w_embed.shape, BF16),
        ],
        scratch_shapes=[
            pltpu.VMEM((count * parts, width), BF16),
            pltpu.SemaphoreType.DMA((2, hidden // block)),
        ],
        compiler_params=params(16),
        name="encode",
    )(content, in_hbm(w_hidden), in_hbm(w_embed))


def project_kernel(
    mine_ref, other_ref, wq_ref, wg_ref, wp_ref, cot_ref, send_ref, gates_ref, og_ref, qs_ref, gs_ref
):
    embedded = (0.5 * (mine_ref[...] + other_ref[...])).astype(BF16)
    query, query_slope = silu_parts(0.5 * matmul(embedded, wq_ref[...]))
    gate, gate_slope = silu_parts(0.5 * matmul(embedded, wg_ref[...]))
    qs_ref[...] = 0.5 * query_slope
    gs_ref[...] = 0.5 * gate_slope
    gates_ref[...] = gate.astype(BF16).astype(F32)
    og_ref[...] = contract_last(cot_ref[...], wp_ref[...]).astype(BF16).astype(F32)
    block = query.reshape(send_ref.shape[1:]).astype(BF16)
    for index in range(send_ref.shape[0]):
        send_ref[index] = block


def project(mine, other, w_query, w_gate, w_proj, cotangent, copies, users):
    count = mine.shape[0]
    local = w_query.shape[1]
    rows = jax.ShapeDtypeStruct((count, local), F32)
    return pl.pallas_call(
        project_kernel,
        out_shape=[jax.ShapeDtypeStruct((copies, users, count // users, local), BF16)] + [rows] * 4,
        compiler_params=params(8),
        name="project",
    )(mine, other, w_query, w_gate, w_proj, cotangent)


def forward_kernel(
    scale,
    heads,
    block,
    query_ref,
    cutoff_ref,
    key_hbm,
    value_hbm,
    out_ref,
    slope_ref,
    key_ref,
    value_ref,
    limit_ref,
    sems,
):
    users, events = key_ref.shape[0], key_ref.shape[1]
    base = lax.axis_index("ctx") * events

    def fetch(user):
        return (
            pltpu.make_async_copy(key_hbm.at[user], key_ref.at[user], sems.at[0, user]),
            pltpu.make_async_copy(value_hbm.at[user], value_ref.at[user], sems.at[1, user]),
        )

    for user in range(min(2, users)):
        for copy in fetch(user):
            copy.start()
    targets, local = query_ref.shape[0] * query_ref.shape[2], query_ref.shape[3]
    half_scale = jnp.asarray(0.5 * scale, F32)
    spots = lax.broadcasted_iota(jnp.int32, (targets, block), 1).astype(F32).astype(BF16)

    def one_user(user, carry):
        queries = query_ref[:, pl.ds(user, 1)].astype(F32).reshape(targets, local).astype(BF16)
        limits = (cutoff_ref[pl.ds(user, 1), :] - base).astype(F32)
        limit_ref[...] = jnp.broadcast_to(limits, (targets, targets)).T

        @pl.when(user + 2 < users)
        def _():
            for copy in fetch(user + 2):
                copy.start()

        for copy in fetch(user):
            copy.wait()
        totals = [jnp.zeros((targets, DH), F32) for _ in range(heads)]
        for start in range(0, events, block):
            rows = slice(start, start + block)
            left = jnp.broadcast_to(limit_ref[:, 0:1] - float(start), (targets, block)).astype(BF16)
            visible = spots < left
            for head in range(heads):
                lanes = slice(head * DH, (head + 1) * DH)
                raw = contract_last(queries[:, lanes], key_ref[user, rows, lanes])
                half = (raw * half_scale).astype(BF16)
                tanh = jnp.where(visible, jnp.tanh(half), jnp.asarray(-1.0, BF16))
                lift = jnp.asarray(1.0, BF16) + tanh
                weights = half * lift
                slope_ref[user, head, :, rows] = lift + weights * (jnp.asarray(1.0, BF16) - tanh)
                totals[head] = totals[head] + matmul(weights, value_ref[user, rows, lanes])
        total = jnp.concatenate(totals, axis=-1)
        out_ref[:, pl.ds(user, 1)] = total.reshape(-1, 1, query_ref.shape[2], local).astype(BF16)
        return carry

    lax.fori_loop(0, users, one_user, 0)


def forward_attention(queries, cutoffs, keys, values, heads):
    copies, users, rows, local = queries.shape
    events = keys.shape[1]
    targets = copies * rows
    return pl.pallas_call(
        functools.partial(forward_kernel, DH ** (-0.5), heads, chunk_of(events, 256)),
        in_specs=in_vmem(2) + [pl.BlockSpec(memory_space=pltpu.HBM)] * 2,
        out_specs=in_vmem(4),
        out_shape=[
            jax.ShapeDtypeStruct(queries.shape, BF16),
            pltpu.VMEM((users, heads, targets, events), BF16),
            pltpu.VMEM(keys.shape, BF16),
            pltpu.VMEM(values.shape, BF16),
        ],
        scratch_shapes=[
            pltpu.VMEM((targets, targets), F32),
            pltpu.SemaphoreType.DMA((2, users)),
        ],
        compiler_params=params(16),
        name="attention_forward",
    )(queries, cutoffs, in_hbm(keys), in_hbm(values))


def norm_kernel(heads, parts_ref, gates_ref, og_ref, send_ref, gg_ref):
    total = parts_ref[0].astype(F32)
    for index in range(1, parts_ref.shape[0]):
        total = total + parts_ref[index].astype(F32)
    attended = total.reshape(gates_ref.shape)
    pieces = []
    for head in range(heads):
        lanes = slice(head * DH, (head + 1) * DH)
        rows = attended[:, lanes]
        rscale = lax.rsqrt(jnp.mean(rows * rows, axis=-1, keepdims=True) + 1e-06)
        normed = rows * rscale
        out_grad = og_ref[:, lanes]
        gg_ref[:, lanes] = out_grad * normed
        normed_grad = out_grad * gates_ref[:, lanes]
        mean = jnp.mean(normed_grad * normed, axis=-1, keepdims=True)
        pieces.append(rscale * (normed_grad - normed * mean))
    grad = jnp.concatenate(pieces, axis=-1)
    block = grad.reshape(send_ref.shape[1:]).astype(BF16)
    for index in range(send_ref.shape[0]):
        send_ref[index] = block


def norm_grads(partials, gates, out_grad, heads):
    return pl.pallas_call(
        functools.partial(norm_kernel, heads),
        out_shape=[
            jax.ShapeDtypeStruct(partials.shape, BF16),
            jax.ShapeDtypeStruct(gates.shape, F32),
        ],
        compiler_params=params(8),
        name="norm_grads",
    )(partials, gates, out_grad)


def backward_kernel(scale, heads, block, grad_ref, slope_ref, key_ref, value_ref, out_ref):
    users, events = key_ref.shape[0], key_ref.shape[1]
    targets, local = grad_ref.shape[0] * grad_ref.shape[2], grad_ref.shape[3]

    def one_user(user, carry):
        grads = grad_ref[:, pl.ds(user, 1)].astype(F32).reshape(targets, local).astype(BF16)
        totals = [jnp.zeros((targets, DH), F32) for _ in range(heads)]
        for start in range(0, events, block):
            rows = slice(start, start + block)
            for head in range(heads):
                lanes = slice(head * DH, (head + 1) * DH)
                weight_grad = contract_last(grads[:, lanes], value_ref[user, rows, lanes])
                grad_scores = weight_grad.astype(BF16) * slope_ref[user, head, :, rows]
                totals[head] = totals[head] + matmul(grad_scores, key_ref[user, rows, lanes])
        total = jnp.concatenate(totals, axis=-1) * (0.5 * scale)
        out_ref[:, pl.ds(user, 1)] = total.reshape(-1, 1, grad_ref.shape[2], local).astype(BF16)
        return carry

    lax.fori_loop(0, users, one_user, 0)


def backward_attention(grads, slopes, keys, values, heads):
    return pl.pallas_call(
        functools.partial(backward_kernel, DH ** (-0.5), heads, chunk_of(keys.shape[1], 256)),
        in_specs=in_vmem(4),
        out_specs=in_vmem(1)[0],
        out_shape=jax.ShapeDtypeStruct(grads.shape, BF16),
        compiler_params=params(16),
        name="attention_backward",
    )(grads, kept_in_vmem(slopes), kept_in_vmem(keys), kept_in_vmem(values))


def embed_kernel(parts_ref, gg_ref, qs_ref, gs_ref, wq_ref, wg_ref, out_ref):
    total = parts_ref[0].astype(F32)
    for index in range(1, parts_ref.shape[0]):
        total = total + parts_ref[index].astype(F32)
    query_back = (total.reshape(qs_ref.shape) * qs_ref[...]).astype(BF16)
    gate_back = (gg_ref[...] * gs_ref[...]).astype(BF16)
    out_ref[...] = contract_last(query_back, wq_ref[...]) + contract_last(gate_back, wg_ref[...])


def embed_grads(partials, gate_grad, query_slope, gate_slope, w_query, w_gate):
    return pl.pallas_call(
        embed_kernel,
        out_shape=jax.ShapeDtypeStruct((gate_grad.shape[0], w_query.shape[0]), F32),
        compiler_params=params(8),
        name="embed_grads",
    )(partials, gate_grad, query_slope, gate_slope, w_query, w_gate)


def content_kernel(parts, block, mine_ref, other_ref, we_ref, slope_ref, wh_ref, keep_ref, send_ref, back_ref):
    count = mine_ref.shape[0]
    half = parts // 2
    kept = half * count
    embed_grad = (0.5 * (mine_ref[...] + other_ref[...])).astype(BF16)
    hidden_grad = 0.5 * contract_last(embed_grad, we_ref[...])
    head = lax.axis_index("head")
    for index in range(parts):
        side = head if index < half else 1 - head
        source = pl.multiple_of((side * half + index % half) * count, count)
        back_ref[index * count : (index + 1) * count] = (
            hidden_grad * slope_ref[pl.ds(source, count), :]
        ).astype(BF16)
    for start in range(0, wh_ref.shape[0], block):
        columns = slice(start, start + block)
        part = contract_last(back_ref[...], wh_ref[columns, :])
        keep_ref[:, columns] = part[:kept]
        send_ref[:, columns] = part[kept:].astype(BF16)


def content_grads(mine, other, w_embed, slopes, w_hidden, parts, block):
    count, hidden = slopes.shape
    width = w_hidden.shape[0]
    return pl.pallas_call(
        functools.partial(content_kernel, parts, block),
        in_specs=in_vmem(5),
        out_specs=in_vmem(2),
        out_shape=[
            jax.ShapeDtypeStruct((count // 2, width), F32),
            jax.ShapeDtypeStruct((count // 2, width), BF16),
        ],
        scratch_shapes=[pltpu.VMEM((count, hidden), BF16)],
        compiler_params=params(16),
        name="content_grads",
    )(mine, other, kept_in_vmem(w_embed), kept_in_vmem(slopes), kept_in_vmem(w_hidden))


def body(
    head_count,
    content_rows,
    w_hidden,
    w_embed,
    w_query,
    w_gate,
    w_proj,
    history_keys,
    history_values,
    cutoffs,
    out_cotangent,
):
    users, shard_rows, parts, width = content_rows.shape
    local = w_query.shape[1]
    heads = local // DH
    count = users * shard_rows
    copies = cutoffs.shape[1] // shard_rows
    swap = [(index, (index + 1) % head_count) for index in range(head_count)]

    def to_owner(blocks):
        return lax.all_to_all(blocks, "ctx", 0, 0, tiled=True)

    hidden_slope, mine, w_hidden, w_embed = encode(
        content_rows.reshape(count, parts, width), w_hidden, w_embed, 256
    )
    other = lax.ppermute(mine, "head", swap)
    cotangent = out_cotangent.reshape(count, -1)
    sends, gates, out_grad, query_slope, gate_slope = project(
        mine, other, w_query, w_gate, w_proj, cotangent, copies, users
    )
    queries = to_owner(sends)
    partial, slopes, history_keys, history_values = forward_attention(
        queries, cutoffs, history_keys, history_values, heads
    )
    sends, gate_grad = norm_grads(to_owner(partial), gates, out_grad, heads)
    grads = to_owner(sends)
    partial = backward_attention(grads, slopes, history_keys, history_values, heads)
    mine = embed_grads(to_owner(partial), gate_grad, query_slope, gate_slope, w_query, w_gate)
    other = lax.ppermute(mine, "head", swap)
    keep, send = content_grads(
        mine, other, w_embed, hidden_slope, w_hidden, parts, 256
    )
    got = lax.ppermute(send, "head", swap)
    total = (keep + got.astype(F32)).astype(BF16)
    half = parts // head_count
    return total.reshape(half, count, width).transpose(1, 0, 2).reshape(users, shard_rows, half, width)


def solution(mesh):
    in_specs = (
        P(None, "ctx", None, None),
        P(None, "head"),
        P("head", None),
        P(None, "head"),
        P(None, "head"),
        P("head", None),
        P(None, "ctx", "head"),
        P(None, "ctx", "head"),
        P(),
        P(None, "ctx", None),
    )
    out_specs = P(None, "ctx", "head", None)
    return jax.shard_map(
        functools.partial(body, mesh.shape["head"]),
        mesh=mesh,
        in_specs=in_specs,
        out_specs=out_specs,
        check_vma=False,
    )
```

time: 109 us -> 84 us (0.77)
  blocking collectives: 37.9 us -> 56.1 us
  Pallas kernels: 33.9 us -> 21 us
  local copies, waits for them, and re-layouts: 13.2 us -> 2.03 us
  waiting for transfers between devices: 13.5 us -> 3.54 us
  starting transfers between devices: 8.99 us -> 0.78 us
    all_to_all x3 -> x4, blocking collectives: 37.9 us -> 56.1 us  [to_owner(): return lax.all_to_all(blocks, 'ctx', 0, 0, tiled=True)]
    pallas_call x4, Pallas kernels: 32.5 us -> 20.3 us  [the longest x1 6.64 us: forward_attention(): pl.pallas_call(functools.partial(forward_kernel, DH ** (-0.5), heads, chu...]
    all_to_all x1 -> x0, waiting for transfers between devices: 10 us -> none  [to_owner(): return lax.all_to_all(blocks, 'ctx', 0, 0, tiled=True)]
    unnamed x24 -> x12, local copies, waits for them, and re-layouts: 10.7 us -> 1.06 us
    all_to_all x1 -> x0, starting transfers between devices: 8.21 us -> none  [to_owner(): return lax.all_to_all(blocks, 'ctx', 0, 0, tiled=True)]
    reshape x1 -> x0, local copies, waits for them, and re-layouts: 1.33 us -> none  [body(): content_rows.reshape(count, parts, width).transpose(1, 0, 2)]
  transfers between devices with their start and end apart: 4 -> 3, of which waited for: 4 -> 3; matrix products, arithmetic and copies ran while one was open for 0% -> 0% of each run, Pallas kernels for 0% -> 0%
where the time goes in v2:
time: 84 us; the launch traced here: 83.7 us
  blocking collectives  56.1 us (67%)
  Pallas kernels  21 us (25%)
  waiting for transfers between devices  3.54 us (4%)
  local copies, waits for them, and re-layouts  2.03 us (2%)
    all_to_all x4, blocking collectives, to_owner(): return lax.all_to_all(blocks, 'ctx', 0, 0, tiled=True)  56.1 us
    pallas_call x1, Pallas kernels, forward_attention(): pl.pallas_call(functools.partial(forward_kernel, DH ** (-0.5), heads, chu...  6.64 us
    pallas_call x1, Pallas kernels, encode(): pl.pallas_call(functools.partial(encode_kernel, parts, block), in_specs=i...  5.71 us
    pallas_call x1, Pallas kernels, backward_attention(): pl.pallas_call(functools.partial(backward_kernel, DH ** (-0.5), heads, ch...  4.44 us
    pallas_call x1, Pallas kernels, content_grads(): pl.pallas_call(functools.partial(content_kernel, parts, block), in_specs=...  3.47 us
    ppermute x2, waiting for transfers between devices, body(): other = lax.ppermute(mine, 'head', swap)  2.16 us
  transfers between devices with their start and end apart: 3, of which 3 were waited for; matrix products, arithmetic and copies ran while one was open for 0% of the time, Pallas kernels for 0%

profile of v2, /device:TPU:0, one launch (start us, length us, event | category | flops | bytes accessed | tf_op | source)
XLA Modules:
  0.0 83.7 jit_solution(5060460180626104955)
XLA Ops:
  0.0 0.0 copy-start.2
  0.0 1.0 %copy-done.2 = bf16[4,8,4,2048]{3,2,1,0:T(4,128)(2,1)S(1)} copy-done((bf16[4,8,4,2048]{3,2,1,0:T(4,128)(2,1)S(1)}, bf16[4,8,4,2048]{3,2,1,0:T(4,128)(2,1)}, u32[]{:S(2)}) %copy-start.2) | copy-done | bytes 524312
  1.0 0.0 copy-start
  1.0 0.0 copy-start.1
  1.0 0.0 copy-start.3
  1.0 0.0 copy-start.4
  1.1 0.0 copy-start.5
  1.1 5.7 %encode.1 = (f32[128,2048]{1,0:T(8,128)S(1)}, f32[32,512]{1,0:T(8,128)S(1)}, bf16[2048,2048]{1,0:T(8,128)(2,1)S(1)}, bf16[2048,512]{1,0:T(8,128)(2,1)S(1)}) custom-call(bf16[32,4,2048]{2,1,0:T(4,128)(2,1)S(1)} %bitcast.6, bf16[2048,2048]{1,0:T(8,128)(2,1)} %wh_hbm.1, bf16[2048,512]{1,0:T(8,128)(2,1)} %we_hbm.1), custom_call_target="tpu_custom_call" | custom-call | tf_op jit(solution)/shard_map/encode/pallas_call | solution.py:93
  6.8 0.6 collective-permute-start
  7.3 0.9 %collective-permute-done.other_ref = f32[32,512]{1,0:T(8,128)S(1)} collective-permute-done((f32[32,512]{1,0:T(8,128)S(1)}, f32[32,512]{1,0:T(8,128)S(1)}, u32[]{:S(2)}, u32[]{:S(2)}) %collective-permute-start) | collective-permute-done | bytes 65568 | tf_op jit(solution)/shard_map/ppermute | solution.py:373
  8.2 0.0 copy-done
  8.2 0.0 copy-done.1
  8.2 0.0 copy-done.3
  8.2 0.0 copy-done.4
  8.3 0.3 project.1
  8.5 18.2 %all_to_all.20.query_ref = bf16[16,4,8,256]{3,2,1,0:T(8,128)(2,1)S(1)} all-to-all(bf16[16,4,8,256]{3,2,1,0:T(8,128)(2,1)S(1)} %get-tuple-element.23), channel_id=1, replica_groups=mesh['ctx'=16,'head'=2] {'ctx'}, dimensions={0} | all-to-all | bytes 524288 | tf_op jit(solution)/shard_map/all_to_all | solution.py:368
  26.7 0.0 copy-done.5
  26.7 6.6 %attention_forward.1 = (bf16[16,4,8,256]{3,2,1,0:T(8,128)(2,1)S(1)}, bf16[4,2,128,2304]{3,2,1,0:T(8,128)(2,1)S(1)}, bf16[4,2304,256]{2,1,0:T(8,128)(2,1)S(1)}, bf16[4,2304,256]{2,1,0:T(8,128)(2,1)S(1)}) custom-call(bf16[16,4,8,256]{3,2,1,0:T(8,128)(2,1)S(1)} %all_to_all.20.query_ref, s32[4,128]{1,0:T(4,128)S(1)} %copy-done.5, bf16[4,2304,256]{2,1,0:T(8,128)(2,1)} %key_hbm.1, ...), custom_call_target="tpu_custom_call" | custom-call | tf_op jit(solution)/shard_map/attention_forward/pallas_call | solution.py:207
  33.4 12.8 %all_to_all.21.parts_ref = bf16[16,4,8,256]{3,2,1,0:T(8,128)(2,1)S(1)} all-to-all(bf16[16,4,8,256]{3,2,1,0:T(8,128)(2,1)S(1)} %get-tuple-element.24), channel_id=1, replica_groups=mesh['ctx'=16,'head'=2] {'ctx'}, dimensions={0} | all-to-all | bytes 524288 | tf_op jit(solution)/shard_map/all_to_all | solution.py:368
  46.2 0.2 norm_grads.1
  46.4 12.6 %all_to_all.22.grad_ref = bf16[16,4,8,256]{3,2,1,0:T(8,128)(2,1)S(1)} all-to-all(bf16[16,4,8,256]{3,2,1,0:T(8,128)(2,1)S(1)} %get-tuple-element.27), channel_id=1, replica_groups=mesh['ctx'=16,'head'=2] {'ctx'}, dimensions={0} | all-to-all | bytes 524288 | tf_op jit(solution)/shard_map/all_to_all | solution.py:368
  59.0 4.4 %attention_backward.1 = bf16[16,4,8,256]{3,2,1,0:T(8,128)(2,1)S(1)} custom-call(bf16[16,4,8,256]{3,2,1,0:T(8,128)(2,1)S(1)} %all_to_all.22.grad_ref, bf16[4,2,128,2304]{3,2,1,0:T(8,128)(2,1)S(1)} %get-tuple-element.28.slope_ref, bf16[4,2304,256]{2,1,0:T(8,128)(2,1)S(1)} %get-tuple-element.29.key_ref, bf16[4,2304,256]{2,1,0:T(8,128)(2,1)S(1)} %get-tuple-element.30.value_ref), custom_call_target="tpu_custom_call" | custom-call | tf_op jit(solution)/shard_map/attention_backward/pallas_call | solution.py:282
  63.5 12.5 %all_to_all.23.parts_ref = bf16[16,4,8,256]{3,2,1,0:T(8,128)(2,1)S(1)} all-to-all(bf16[16,4,8,256]{3,2,1,0:T(8,128)(2,1)S(1)} %attention_backward.1), channel_id=1, replica_groups=mesh['ctx'=16,'head'=2] {'ctx'}, dimensions={0} | all-to-all | bytes 524288 | tf_op jit(solution)/shard_map/all_to_all | solution.py:368
  76.0 0.3 embed_grads.1.mine_ref
  76.3 0.0 collective-permute-start.1
  76.3 1.3 %collective-permute-done.1.other_ref = f32[32,512]{1,0:T(8,128)S(1)} collective-permute-done((f32[32,512]{1,0:T(8,128)S(1)}, f32[32,512]{1,0:T(8,128)S(1)}, u32[]{:S(2)}, u32[]{:S(2)}) %collective-permute-start.1) | collective-permute-done | bytes 65568 | tf_op jit(solution)/shard_map/ppermute | solution.py:386
  77.5 3.5 %content_grads.1 = (f32[64,2048]{1,0:T(8,128)S(1)}, bf16[64,2048]{1,0:T(8,128)(2,1)S(1)}) custom-call(f32[32,512]{1,0:T(8,128)S(1)} %embed_grads.1.mine_ref, f32[32,512]{1,0:T(8,128)S(1)} %collective-permute-done.1.other_ref, bf16[2048,512]{1,0:T(8,128)(2,1)S(1)} %get-tuple-element.34.we_ref, f32[128,2048]{1,0:T(8,128)S(1)} %get-tuple-element.35.slope_ref, ...), custom_call_target="tpu_custom_call" | custom-call | tf_op jit(solution)/shard_map/content_grads/pallas_call | solution.py:333
  81.0 0.2 collective-permute-start.2
  81.2 1.4 %collective-permute-done.2 = bf16[64,2048]{1,0:T(8,128)(2,1)S(1)} collective-permute-done((bf16[64,2048]{1,0:T(8,128)(2,1)S(1)}, bf16[64,2048]{1,0:T(8,128)(2,1)S(1)}, u32[]{:S(2)}, u32[]{:S(2)}) %collective-permute-start.2) | collective-permute-done | bytes 262176 | tf_op jit(solution)/shard_map/ppermute | solution.py:390
  82.6 0.1 add_convert_fusion
  82.7 1.0 %copy.11 = bf16[32,2,2048]{2,1,0:T(2,128)(2,1)} copy(bf16[32,2,2048]{2,0,1:T(8,128)(2,1)S(1)} %bitcast.8) | data formatting | bytes 524288 | tf_op jit(solution)/shard_map/transpose | solution.py:393
Async XLA Ops:
  0.0 1.0 %copy-start.2 = (bf16[4,8,4,2048]{3,2,1,0:T(4,128)(2,1)S(1)}, bf16[4,8,4,2048]{3,2,1,0:T(4,128)(2,1)}, u32[]{:S(2)}) copy-start(bf16[4,8,4,2048]{3,2,1,0:T(4,128)(2,1)} %param.10) | copy-start | bytes 1572868
  1.0 7.2 %copy-start = (bf16[512,256]{1,0:T(8,128)(2,1)S(1)}, bf16[512,256]{1,0:T(8,128)(2,1)}, u32[]{:S(2)}) copy-start(bf16[512,256]{1,0:T(8,128)(2,1)} %wq_ref.3) | copy-start | bytes 786436
  1.0 7.2 %copy-start.1 = (bf16[512,256]{1,0:T(8,128)(2,1)S(1)}, bf16[512,256]{1,0:T(8,128)(2,1)}, u32[]{:S(2)}) copy-start(bf16[512,256]{1,0:T(8,128)(2,1)} %wg_ref.3) | copy-start | bytes 786436
  1.0 7.2 %copy-start.3 = (bf16[256,512]{1,0:T(8,128)(2,1)S(1)}, bf16[256,512]{1,0:T(8,128)(2,1)}, u32[]{:S(2)}) copy-start(bf16[256,512]{1,0:T(8,128)(2,1)} %wp_ref.1) | copy-start | bytes 786436
  1.0 7.2 %copy-start.4 = (bf16[4,8,512]{2,1,0:T(8,128)(2,1)S(1)}, bf16[4,8,512]{2,1,0:T(8,128)(2,1)}, u32[]{:S(2)}) copy-start(bf16[4,8,512]{2,1,0:T(8,128)(2,1)} %param.19) | copy-start | bytes 98308
  1.1 25.7 %copy-start.5 = (s32[4,128]{1,0:T(4,128)S(1)}, s32[4,128]{1,0:T(4,128)}, u32[]{:S(2)}) copy-start(s32[4,128]{1,0:T(4,128)} %cutoff_ref.1) | copy-start | bytes 6148
  6.8 1.5 %collective-permute-start = (f32[32,512]{1,0:T(8,128)S(1)}, f32[32,512]{1,0:T(8,128)S(1)}, u32[]{:S(2)}, u32[]{:S(2)}) collective-permute-start(f32[32,512]{1,0:T(8,128)S(1)} %get-tuple-element.22.mine_ref), channel_id=1, source_target_pairs={{0,1},{1,0},{2,3},{3,2},{4,5},{5,4},{6,7},{7,6},{8,9},{9,8},{10,11... | collective-permute-start | bytes 196616 | tf_op jit(solution)/shard_map/ppermute | solution.py:373
  76.3 1.3 %collective-permute-start.1 = (f32[32,512]{1,0:T(8,128)S(1)}, f32[32,512]{1,0:T(8,128)S(1)}, u32[]{:S(2)}, u32[]{:S(2)}) collective-permute-start(f32[32,512]{1,0:T(8,128)S(1)} %embed_grads.1.mine_ref), channel_id=1, source_target_pairs={{0,1},{1,0},{2,3},{3,2},{4,5},{5,4},{6,7},{7,6},{8,9},{9,8},{10,11... | collective-permute-start | bytes 196616 | tf_op jit(solution)/shard_map/ppermute | solution.py:386
  81.0 1.6 %collective-permute-start.2 = (bf16[64,2048]{1,0:T(8,128)(2,1)S(1)}, bf16[64,2048]{1,0:T(8,128)(2,1)S(1)}, u32[]{:S(2)}, u32[]{:S(2)}) collective-permute-start(bf16[64,2048]{1,0:T(8,128)(2,1)S(1)} %get-tuple-element.38), channel_id=1, source_target_pairs={{0,1},{1,0},{2,3},{3,2},{4,5},{5,4},{6,7},{7,6},{8,9},{9,8},{10,11... | collective-permute-start | bytes 786440 | tf_op jit(solution)/shard_map/ppermute | solution.py:390

commit v3 on v2

v3 whole, which is shorter than its diff:
```python
import functools

import jax
import jax.numpy as jnp
from jax import lax
from jax.experimental import pallas as pl
from jax.experimental.pallas import tpu as pltpu
from jax.sharding import PartitionSpec as P


DH = 128
F32 = jnp.float32
BF16 = jnp.bfloat16
GROUP = 9


def matmul(left, right):
    return jnp.dot(left, right, preferred_element_type=F32)


def contract_last(left, right):
    return lax.dot_general(left, right, (((1,), (1,)), ((), ())), preferred_element_type=F32)


def silu_parts(half):
    tanh = jnp.tanh(half)
    lift = 1.0 + tanh
    value = half * lift
    return value, lift + value * (1.0 - tanh)


def params(mebibytes):
    return pltpu.CompilerParams(vmem_limit_bytes=mebibytes << 20)


def in_vmem(count):
    return [pl.BlockSpec(memory_space=pltpu.VMEM)] * count


def in_hbm(array):
    return pltpu.with_memory_space_constraint(array, pltpu.HBM)


def kept_in_vmem(array):
    return pltpu.with_memory_space_constraint(array, pltpu.VMEM)


def chunks_of(length):
    block = 256
    while length % block:
        block //= 2
    group = GROUP
    while (length // block) % group:
        group -= 1
    return block, group


def encode_kernel(
    parts, block, depth, rows_hbm, wh_hbm, we_hbm, slope_ref, out_ref, wh_ref, we_ref, rows_ref, rm_ref, sems, row_sem
):
    total_rows, hidden = slope_ref.shape
    blocks = hidden // block
    count = total_rows // parts
    copies = []
    for index in range(blocks):
        columns = pl.ds(index * block, block)
        copies.append(
            (
                pltpu.make_async_copy(wh_hbm.at[:, columns], wh_ref.at[:, columns], sems.at[0, index]),
                pltpu.make_async_copy(we_hbm.at[columns, :], we_ref.at[columns, :], sems.at[1, index]),
            )
        )
    rows_copy = pltpu.make_async_copy(rows_hbm, rows_ref, row_sem)
    rows_copy.start()
    for pair in copies[:depth]:
        pair[0].start()
        pair[1].start()
    spot = lax.broadcasted_iota(jnp.int32, (total_rows, total_rows), 0)
    from_row = lax.broadcasted_iota(jnp.int32, (total_rows, total_rows), 1)
    wanted = (spot % count) * parts + spot // count
    order = jnp.where(from_row == wanted, 1.0, 0.0).astype(BF16)
    rows_copy.wait()
    rows = rows_ref[...].astype(F32).reshape(total_rows, rows_ref.shape[2]).astype(BF16)
    rm_ref[...] = matmul(order, rows).astype(BF16)
    total = jnp.zeros((total_rows, we_ref.shape[1]), F32)
    for index in range(blocks):
        columns = slice(index * block, (index + 1) * block)
        if index + depth < blocks:
            copies[index + depth][0].start()
            copies[index + depth][1].start()
        copies[index][0].wait()
        lin = matmul(rm_ref[...], wh_ref[:, columns])
        value, slope = silu_parts(0.5 * lin)
        slope_ref[:, columns] = slope
        copies[index][1].wait()
        total = total + matmul(value.astype(BF16), we_ref[columns, :])
    summed = total[0:count]
    for part in range(1, parts):
        summed = summed + total[part * count : (part + 1) * count]
    out_ref[...] = summed


def encode(content, w_hidden, w_embed, block):
    count, parts, width = content.shape
    hidden = w_hidden.shape[1]
    model = w_embed.shape[1]
    return pl.pallas_call(
        functools.partial(encode_kernel, parts, block, 3),
        in_specs=[pl.BlockSpec(memory_space=pltpu.HBM)] * 3,
        out_specs=in_vmem(4),
        out_shape=[
            pltpu.VMEM((count * parts, hidden), F32),
            jax.ShapeDtypeStruct((count, model), F32),
            pltpu.VMEM(w_hidden.shape, BF16),
            pltpu.VMEM(w_embed.shape, BF16),
        ],
        scratch_shapes=[
            pltpu.VMEM(content.shape, BF16),
            pltpu.VMEM((count * parts, width), BF16),
            pltpu.SemaphoreType.DMA((2, hidden // block)),
            pltpu.SemaphoreType.DMA,
        ],
        compiler_params=params(16),
        name="encode",
    )(in_hbm(content), in_hbm(w_hidden), in_hbm(w_embed))


def warm_kernel(after_ref, cot_ref, wp_ref, key_hbm, value_hbm, og_ref, key_ref, value_ref, sems):
    copies = (
        pltpu.make_async_copy(key_hbm.at[0], key_ref, sems.at[0]),
        pltpu.make_async_copy(value_hbm.at[0], value_ref, sems.at[1]),
    )
    for copy in copies:
        copy.start()
    og_ref[...] = contract_last(cot_ref[...], wp_ref[...]).astype(BF16).astype(F32)
    for copy in copies:
        copy.wait()


def warm(after, cotangent, w_proj, keys, values):
    return pl.pallas_call(
        warm_kernel,
        in_specs=in_vmem(3) + [pl.BlockSpec(memory_space=pltpu.HBM)] * 2,
        out_specs=in_vmem(3),
        out_shape=[
            jax.ShapeDtypeStruct((cotangent.shape[0], w_proj.shape[0]), F32),
            pltpu.VMEM(keys.shape[1:], BF16),
            pltpu.VMEM(values.shape[1:], BF16),
        ],
        scratch_shapes=[pltpu.SemaphoreType.DMA((2,))],
        compiler_params=params(8),
        name="warm",
    )(after, cotangent, w_proj, in_hbm(keys), in_hbm(values))


def project_kernel(mine_ref, other_ref, wq_ref, wg_ref, og_ref, send_ref, ng_ref, qs_ref, gs_ref):
    embedded = (0.5 * (mine_ref[...] + other_ref[...])).astype(BF16)
    query, query_slope = silu_parts(0.5 * matmul(embedded, wq_ref[...]))
    gate, gate_slope = silu_parts(0.5 * matmul(embedded, wg_ref[...]))
    qs_ref[...] = 0.5 * query_slope
    gs_ref[...] = 0.5 * gate_slope
    ng_ref[...] = og_ref[...] * gate.astype(BF16).astype(F32)
    block = (query * (0.5 * DH ** (-0.5))).reshape(send_ref.shape[1:]).astype(BF16)
    for index in range(send_ref.shape[0]):
        send_ref[index] = block


def project(mine, other, w_query, w_gate, out_grad, copies, users):
    count = mine.shape[0]
    local = w_query.shape[1]
    rows = jax.ShapeDtypeStruct((count, local), F32)
    return pl.pallas_call(
        project_kernel,
        out_shape=[jax.ShapeDtypeStruct((copies, users, count // users, local), BF16)] + [rows] * 3,
        compiler_params=params(8),
        name="project",
    )(mine, other, w_query, w_gate, out_grad)


def forward_kernel(
    heads,
    block,
    group,
    query_ref,
    cutoff_ref,
    first_key_ref,
    first_value_ref,
    key_hbm,
    value_hbm,
    out_ref,
    slope_ref,
    key_ref,
    value_ref,
    limit_ref,
    sems,
):
    users, events = key_hbm.shape[0], key_hbm.shape[1]
    base = lax.axis_index("ctx") * events

    def fetch(user):
        return (
            pltpu.make_async_copy(key_hbm.at[user], key_ref.at[user - 1], sems.at[0, user - 1]),
            pltpu.make_async_copy(value_hbm.at[user], value_ref.at[user - 1], sems.at[1, user - 1]),
        )

    for user in range(1, min(3, users)):
        for copy in fetch(user):
            copy.start()
    targets, local = query_ref.shape[0] * query_ref.shape[2], query_ref.shape[3]
    one = jnp.asarray(1.0, BF16)
    spots = lax.broadcasted_iota(jnp.int32, (targets, block), 1).astype(F32).astype(BF16)

    for user in range(users):
        queries = query_ref[:, pl.ds(user, 1)].astype(F32).reshape(targets, local).astype(BF16)
        limits = (cutoff_ref[pl.ds(user, 1), :] - base).astype(F32)
        limit_ref[...] = jnp.broadcast_to(limits, (block, targets)).T

        if user == 0:
            keys_here, values_here = first_key_ref, first_value_ref
        else:
            if user + 2 < users:
                for copy in fetch(user + 2):
                    copy.start()
            for copy in fetch(user):
                copy.wait()
            keys_here, values_here = key_ref.at[user - 1], value_ref.at[user - 1]
        totals = [jnp.zeros((targets, DH), F32) for _ in range(heads)]
        for first in range(0, events, block * group):
            span = slice(first, first + block * group)
            for head in range(heads):
                lanes = slice(head * DH, (head + 1) * DH)
                weights = []
                for start in range(first, first + block * group, block):
                    rows = slice(start, start + block)
                    left = (limit_ref[...] - float(start)).astype(BF16)
                    visible = spots < left
                    half = contract_last(queries[:, lanes], keys_here[rows, lanes]).astype(BF16)
                    tanh = jnp.where(visible, jnp.tanh(half), -one)
                    lift = one + tanh
                    weight = half * lift
                    slope_ref[user, head, :, rows] = lift + weight * (one - tanh)
                    weights.append(weight)
                totals[head] = totals[head] + matmul(
                    jnp.concatenate(weights, axis=-1), values_here[span, lanes]
                )
        total = jnp.concatenate(totals, axis=-1)
        out_ref[:, pl.ds(user, 1)] = total.reshape(-1, 1, query_ref.shape[2], local).astype(BF16)


def forward_attention(queries, cutoffs, first_keys, first_values, keys, values, heads):
    copies, users, rows, _ = queries.shape
    events = keys.shape[1]
    targets = copies * rows
    return pl.pallas_call(
        functools.partial(forward_kernel, heads, *chunks_of(events)),
        in_specs=in_vmem(4) + [pl.BlockSpec(memory_space=pltpu.HBM)] * 2,
        out_specs=in_vmem(4),
        out_shape=[
            jax.ShapeDtypeStruct(queries.shape, BF16),
            pltpu.VMEM((users, heads, targets, events), BF16),
            pltpu.VMEM((users - 1,) + keys.shape[1:], BF16),
            pltpu.VMEM((users - 1,) + values.shape[1:], BF16),
        ],
        scratch_shapes=[
            pltpu.VMEM((targets, chunks_of(events)[0]), F32),
            pltpu.SemaphoreType.DMA((2, users - 1)),
        ],
        compiler_params=params(16),
        name="attention_forward",
    )(
        queries,
        cutoffs,
        kept_in_vmem(first_keys),
        kept_in_vmem(first_values),
        in_hbm(keys),
        in_hbm(values),
    )


def norm_kernel(heads, parts_ref, ng_ref, og_ref, send_ref, gg_ref):
    total = parts_ref[0].astype(F32)
    for index in range(1, parts_ref.shape[0]):
        total = total + parts_ref[index].astype(F32)
    attended = total.reshape(ng_ref.shape)
    pieces = []
    for head in range(heads):
        lanes = slice(head * DH, (head + 1) * DH)
        rows = attended[:, lanes]
        rscale = lax.rsqrt(jnp.mean(rows * rows, axis=-1, keepdims=True) + 1e-06)
        normed = rows * rscale
        gg_ref[:, lanes] = og_ref[:, lanes] * normed
        normed_grad = ng_ref[:, lanes]
        mean = jnp.mean(normed_grad * normed, axis=-1, keepdims=True)
        pieces.append(rscale * (normed_grad - normed * mean))
    grad = jnp.concatenate(pieces, axis=-1)
    block = grad.reshape(send_ref.shape[1:]).astype(BF16)
    for index in range(send_ref.shape[0]):
        send_ref[index] = block


def norm_grads(partials, normed_grad, out_grad, heads):
    return pl.pallas_call(
        functools.partial(norm_kernel, heads),
        out_shape=[
            jax.ShapeDtypeStruct(partials.shape, BF16),
            jax.ShapeDtypeStruct(out_grad.shape, F32),
        ],
        compiler_params=params(8),
        name="norm_grads",
    )(partials, normed_grad, out_grad)


def backward_kernel(
    scale, heads, block, group, grad_ref, slope_ref, first_key_ref, first_value_ref, key_ref, value_ref, out_ref
):
    users, events = grad_ref.shape[1], key_ref.shape[1]
    targets, local = grad_ref.shape[0] * grad_ref.shape[2], grad_ref.shape[3]

    for user in range(users):
        if user == 0:
            keys_here, values_here = first_key_ref, first_value_ref
        else:
            keys_here, values_here = key_ref.at[user - 1], value_ref.at[user - 1]
        grads = grad_ref[:, pl.ds(user, 1)].astype(F32).reshape(targets, local).astype(BF16)
        totals = [jnp.zeros((targets, DH), F32) for _ in range(heads)]
        for first in range(0, events, block * group):
            span = slice(first, first + block * group)
            for head in range(heads):
                lanes = slice(head * DH, (head + 1) * DH)
                scored = []
                for start in range(first, first + block * group, block):
                    rows = slice(start, start + block)
                    weight_grad = contract_last(grads[:, lanes], values_here[rows, lanes])
                    scored.append(weight_grad.astype(BF16) * slope_ref[user, head, :, rows])
                totals[head] = totals[head] + matmul(
                    jnp.concatenate(scored, axis=-1), keys_here[span, lanes]
                )
        total = jnp.concatenate(totals, axis=-1) * (0.5 * scale)
        out_ref[:, pl.ds(user, 1)] = total.reshape(-1, 1, grad_ref.shape[2], local).astype(BF16)


def backward_attention(grads, slopes, history, heads):
    return pl.pallas_call(
        functools.partial(backward_kernel, DH ** (-0.5), heads, *chunks_of(slopes.shape[3])),
        in_specs=in_vmem(6),
        out_specs=in_vmem(1)[0],
        out_shape=jax.ShapeDtypeStruct(grads.shape, BF16),
        compiler_params=params(16),
        name="attention_backward",
    )(grads, kept_in_vmem(slopes), *map(kept_in_vmem, history))


def embed_kernel(parts_ref, gg_ref, qs_ref, gs_ref, wq_ref, wg_ref, out_ref):
    total = parts_ref[0].astype(F32)
    for index in range(1, parts_ref.shape[0]):
        total = total + parts_ref[index].astype(F32)
    query_back = (total.reshape(qs_ref.shape) * qs_ref[...]).astype(BF16)
    gate_back = (gg_ref[...] * gs_ref[...]).astype(BF16)
    out_ref[...] = contract_last(query_back, wq_ref[...]) + contract_last(gate_back, wg_ref[...])


def embed_grads(partials, gate_grad, query_slope, gate_slope, w_query, w_gate):
    return pl.pallas_call(
        embed_kernel,
        out_shape=jax.ShapeDtypeStruct((gate_grad.shape[0], w_query.shape[0]), F32),
        compiler_params=params(8),
        name="embed_grads",
    )(partials, gate_grad, query_slope, gate_slope, w_query, w_gate)


def content_first_kernel(parts, block, mine_ref, other_ref, we_ref, slope_ref, wh_ref, keep_ref, send_ref, back_ref):
    count = mine_ref.shape[0]
    half = parts // 2
    embed_grad = (0.5 * (mine_ref[...] + other_ref[...])).astype(BF16)
    hidden_grad = 0.5 * contract_last(embed_grad, we_ref[...])
    head = lax.axis_index("head")
    for index in range(parts):
        side = head if index < half else 1 - head
        source = pl.multiple_of((side * half + index % half) * count, count)
        back_ref[index * count : (index + 1) * count] = (
            hidden_grad * slope_ref[pl.ds(source, count), :]
        ).astype(BF16)
    content_columns(0, block, back_ref, wh_ref, keep_ref, send_ref)


def content_columns(first, block, back_ref, wh_ref, keep_ref, send_ref):
    kept, width = keep_ref.shape
    for start in range(0, width, block):
        columns = slice(start, start + block)
        part = contract_last(back_ref[...], wh_ref[first + start : first + start + block, :])
        keep_ref[:, columns] = part[:kept]
        send_ref[:, columns] = part[kept:].astype(BF16)


def content_second_kernel(block, back_ref, wh_ref, keep_ref, send_ref):
    content_columns(wh_ref.shape[0] // 2, block, back_ref, wh_ref, keep_ref, send_ref)


def content_first(mine, other, w_embed, slopes, w_hidden, parts, block):
    count, hidden = slopes.shape
    shape = (count // 2, w_hidden.shape[0] // 2)
    return pl.pallas_call(
        functools.partial(content_first_kernel, parts, block),
        in_specs=in_vmem(5),
        out_specs=in_vmem(3),
        out_shape=[
            jax.ShapeDtypeStruct(shape, F32),
            jax.ShapeDtypeStruct(shape, BF16),
            pltpu.VMEM((count, hidden), BF16),
        ],
        compiler_params=params(16),
        name="content_first",
    )(mine, other, kept_in_vmem(w_embed), kept_in_vmem(slopes), kept_in_vmem(w_hidden))


def content_second(back, w_hidden, block):
    shape = (back.shape[0] // 2, w_hidden.shape[0] // 2)
    return pl.pallas_call(
        functools.partial(content_second_kernel, block),
        in_specs=in_vmem(2),
        out_specs=in_vmem(2),
        out_shape=[
            jax.ShapeDtypeStruct(shape, F32),
            jax.ShapeDtypeStruct(shape, BF16),
        ],
        compiler_params=params(16),
        name="content_second",
    )(kept_in_vmem(back), kept_in_vmem(w_hidden))


def combine_kernel(keep1_ref, got1_ref, keep2_ref, got2_ref, out_ref):
    count, half, width = out_ref.shape
    rows = count * half
    spot = lax.broadcasted_iota(jnp.int32, (rows, rows), 0)
    from_row = lax.broadcasted_iota(jnp.int32, (rows, rows), 1)
    order = jnp.where(from_row == (spot % half) * count + spot // half, 1.0, 0.0).astype(BF16)
    for first, keep_ref, got_ref in ((0, keep1_ref, got1_ref), (width // 2, keep2_ref, got2_ref)):
        total = (keep_ref[...] + got_ref[...].astype(F32)).astype(BF16)
        placed = matmul(order, total).reshape(count, half, width // 2)
        out_ref[:, :, first : first + width // 2] = placed.astype(BF16)


def combine(pieces, count, half, width):
    return pl.pallas_call(
        combine_kernel,
        in_specs=in_vmem(4),
        out_specs=in_vmem(1)[0],
        out_shape=jax.ShapeDtypeStruct((count, half, width), BF16),
        compiler_params=params(8),
        name="combine",
    )(*pieces)


def body(
    head_count,
    content_rows,
    w_hidden,
    w_embed,
    w_query,
    w_gate,
    w_proj,
    history_keys,
    history_values,
    cutoffs,
    out_cotangent,
):
    users, shard_rows, parts, width = content_rows.shape
    local = w_query.shape[1]
    heads = local // DH
    count = users * shard_rows
    copies = cutoffs.shape[1] // shard_rows
    swap = [(index, (index + 1) % head_count) for index in range(head_count)]

    def to_owner(blocks):
        return lax.all_to_all(blocks, "ctx", 0, 0, tiled=True)

    hidden_slope, mine, w_hidden, w_embed = encode(
        content_rows.reshape(count, parts, width), w_hidden, w_embed, 256
    )
    other = lax.ppermute(mine, "head", swap)
    cotangent = out_cotangent.reshape(count, -1)
    out_grad, first_keys, first_values = warm(mine, cotangent, w_proj, history_keys, history_values)
    sends, normed_grad, query_slope, gate_slope = project(
        mine, other, w_query, w_gate, out_grad, copies, users
    )
    partial, slopes, rest_keys, rest_values = forward_attention(
        to_owner(sends), cutoffs, first_keys, first_values, history_keys, history_values, heads
    )
    sends, gate_grad = norm_grads(to_owner(partial), normed_grad, out_grad, heads)
    history = (first_keys, first_values, rest_keys, rest_values)
    partial = backward_attention(to_owner(sends), slopes, history, heads)
    mine = embed_grads(to_owner(partial), gate_grad, query_slope, gate_slope, w_query, w_gate)
    other = lax.ppermute(mine, "head", swap)
    keep1, send1, back = content_first(mine, other, w_embed, hidden_slope, w_hidden, parts, 256)
    got1 = lax.ppermute(send1, "head", swap)
    keep2, send2 = content_second(back, w_hidden, 256)
    got2 = lax.ppermute(send2, "head", swap)
    half = parts // head_count
    total = combine((keep1, got1, keep2, got2), count, half, width)
    return total.reshape(users, shard_rows, half, width)


def solution(mesh):
    in_specs = (
        P(None, "ctx", None, None),
        P(None, "head"),
        P("head", None),
        P(None, "head"),
        P(None, "head"),
        P("head", None),
        P(None, "ctx", "head"),
        P(None, "ctx", "head"),
        P(),
        P(None, "ctx", None),
    )
    out_specs = P(None, "ctx", "head", None)
    return jax.shard_map(
        functools.partial(body, mesh.shape["head"]),
        mesh=mesh,
        in_specs=in_specs,
        out_specs=out_specs,
        check_vma=False,
    )
```

time: 84 us -> 81.2 us (0.967)
  local copies, waits for them, and re-layouts: 2.03 us -> 0.02 us
  waiting for transfers between devices: 3.54 us -> 2.29 us
    unnamed x12 -> x10, local copies, waits for them, and re-layouts: 1.06 us -> 0.02 us
    transpose x1 -> x0, local copies, waits for them, and re-layouts: 0.97 us -> none  [body(): total.reshape(half, count, width).transpose(1, 0, 2)]
    ppermute x2, waiting for transfers between devices: 2.16 us -> 1.26 us  [body(): other = lax.ppermute(mine, 'head', swap)]
    pallas_call x4 -> x7, Pallas kernels: 20.3 us -> 20.4 us  [the longest x1 6.92 us: encode(): pl.pallas_call(functools.partial(encode_kernel, parts, block, 3), in_spec...]
  transfers between devices with their start and end apart: 3 -> 4, of which waited for: 3 -> 3; matrix products, arithmetic and copies ran while one was open for 0% -> 0% of each run, Pallas kernels for 0% -> 2%
where the time goes in v3:
time: 81.2 us; the launch traced here: 80.9 us
  blocking collectives  56.2 us (69%)
  Pallas kernels  21.1 us (26%)
  waiting for transfers between devices  2.29 us (3%)
  starting transfers between devices  1.14 us (1%)
    all_to_all x4, blocking collectives, to_owner(): return lax.all_to_all(blocks, 'ctx', 0, 0, tiled=True)  56.2 us
    pallas_call x1, Pallas kernels, encode(): pl.pallas_call(functools.partial(encode_kernel, parts, block, 3), in_spec...  6.92 us
    pallas_call x1, Pallas kernels, forward_attention(): pl.pallas_call(functools.partial(forward_kernel, heads, *chunks_of(events...  4.38 us
    pallas_call x1, Pallas kernels, backward_attention(): pl.pallas_call(functools.partial(backward_kernel, DH ** (-0.5), heads, *c...  2.67 us
    pallas_call x1, Pallas kernels, content_first(): pl.pallas_call(functools.partial(content_first_kernel, parts, block), in_...  2.13 us
    pallas_call x1, Pallas kernels, warm(): pl.pallas_call(warm_kernel, in_specs=in_vmem(3) + [pl.BlockSpec(memory_sp...  1.71 us
  transfers between devices with their start and end apart: 4, of which 3 were waited for; matrix products, arithmetic and copies ran while one was open for 0% of the time, Pallas kernels for 2%

profile of v3, /device:TPU:0, one launch (start us, length us, event | category | flops | bytes accessed | tf_op | source)
XLA Modules:
  0.0 80.9 jit_solution(14318174216955698427)
XLA Ops:
  0.0 0.0 copy-start.2
  0.0 0.0 copy-start.3
  0.0 6.9 %encode.1 = (f32[128,2048]{1,0:T(8,128)S(1)}, f32[32,512]{1,0:T(8,128)S(1)}, bf16[2048,2048]{1,0:T(8,128)(2,1)S(1)}, bf16[2048,512]{1,0:T(8,128)(2,1)S(1)}) custom-call(bf16[32,4,2048]{2,1,0:T(4,128)(2,1)} %bitcast.4, bf16[2048,2048]{1,0:T(8,128)(2,1)} %wh_hbm.1, bf16[2048,512]{1,0:T(8,128)(2,1)} %we_hbm.1), custom_call_target="tpu_custom_call" | custom-call | tf_op jit(solution)/shard_map/encode/pallas_call | solution.py:107
  6.9 0.6 collective-permute-start
  7.5 0.0 copy-done.2
  7.5 0.0 copy-done.3
  7.5 0.0 copy-start
  7.5 0.0 copy-start.1
  7.5 0.0 copy-start.4
  7.5 1.7 %warm.1 = (f32[32,256]{1,0:T(8,128)S(1)}, bf16[2304,256]{1,0:T(8,128)(2,1)S(1)}, bf16[2304,256]{1,0:T(8,128)(2,1)S(1)}) custom-call(f32[32,512]{1,0:T(8,128)S(1)} %get-tuple-element.27.after_ref.mine_ref, bf16[32,512]{1,0:T(8,128)(2,1)S(1)} %bitcast.3, bf16[256,512]{1,0:T(8,128)(2,1)S(1)} %copy-done.2, bf16[4,2304,256]{2,1,0:T(8,128)(2,1)} %key_hbm.3, ...), custom_call_target="tpu_custom_call" | custom-call | tf_op jit(solution)/shard_map/warm/pallas_call | solution.py:141
  9.2 0.0 collective-permute-done.other_ref
  9.2 0.0 copy-done
  9.3 0.0 copy-done.1
  9.3 0.2 project.1
  9.5 18.2 %all_to_all.20.query_ref = bf16[16,4,8,256]{3,2,1,0:T(8,128)(2,1)S(1)} all-to-all(bf16[16,4,8,256]{3,2,1,0:T(8,128)(2,1)S(1)} %get-tuple-element.29), channel_id=1, replica_groups=mesh['ctx'=16,'head'=2] {'ctx'}, dimensions={0} | all-to-all | bytes 524288 | tf_op jit(solution)/shard_map/all_to_all | solution.py:475
  27.7 0.0 copy-done.4
  27.7 4.4 %attention_forward.1 = (bf16[16,4,8,256]{3,2,1,0:T(8,128)(2,1)S(1)}, bf16[4,2,128,2304]{3,2,1,0:T(8,128)(2,1)S(1)}, bf16[3,2304,256]{2,1,0:T(8,128)(2,1)S(1)}, bf16[3,2304,256]{2,1,0:T(8,128)(2,1)S(1)}) custom-call(bf16[16,4,8,256]{3,2,1,0:T(8,128)(2,1)S(1)} %all_to_all.20.query_ref, s32[4,128]{1,0:T(4,128)S(1)} %copy-done.4, ...), custom_call_target="tpu_custom_call" | custom-call | tf_op jit(solution)/shard_map/attention_forward/pallas_call | solution.py:254
  32.1 12.8 %all_to_all.21.parts_ref = bf16[16,4,8,256]{3,2,1,0:T(8,128)(2,1)S(1)} all-to-all(bf16[16,4,8,256]{3,2,1,0:T(8,128)(2,1)S(1)} %get-tuple-element.32), channel_id=1, replica_groups=mesh['ctx'=16,'head'=2] {'ctx'}, dimensions={0} | all-to-all | bytes 524288 | tf_op jit(solution)/shard_map/all_to_all | solution.py:475
  44.9 0.2 norm_grads.1
  45.2 12.6 %all_to_all.22.grad_ref = bf16[16,4,8,256]{3,2,1,0:T(8,128)(2,1)S(1)} all-to-all(bf16[16,4,8,256]{3,2,1,0:T(8,128)(2,1)S(1)} %get-tuple-element.34), channel_id=1, replica_groups=mesh['ctx'=16,'head'=2] {'ctx'}, dimensions={0} | all-to-all | bytes 524288 | tf_op jit(solution)/shard_map/all_to_all | solution.py:475
  57.8 2.7 %attention_backward.1 = bf16[16,4,8,256]{3,2,1,0:T(8,128)(2,1)S(1)} custom-call(bf16[16,4,8,256]{3,2,1,0:T(8,128)(2,1)S(1)} %all_to_all.22.grad_ref, bf16[4,2,128,2304]{3,2,1,0:T(8,128)(2,1)S(1)} %get-tuple-element.35.slope_ref, bf16[2304,256]{1,0:T(8,128)(2,1)S(1)} %get-tuple-element.30.first_key_ref, ...), custom_call_target="tpu_custom_call" | custom-call | tf_op jit(solution)/shard_map/attention_backward/pallas_call | solution.py:343
  60.4 12.5 %all_to_all.23.parts_ref = bf16[16,4,8,256]{3,2,1,0:T(8,128)(2,1)S(1)} all-to-all(bf16[16,4,8,256]{3,2,1,0:T(8,128)(2,1)S(1)} %attention_backward.1), channel_id=1, replica_groups=mesh['ctx'=16,'head'=2] {'ctx'}, dimensions={0} | all-to-all | bytes 524288 | tf_op jit(solution)/shard_map/all_to_all | solution.py:475
  73.0 0.3 embed_grads.1.mine_ref
  73.2 0.0 collective-permute-start.1
  73.2 1.3 %collective-permute-done.1.other_ref = f32[32,512]{1,0:T(8,128)S(1)} collective-permute-done((f32[32,512]{1,0:T(8,128)S(1)}, f32[32,512]{1,0:T(8,128)S(1)}, u32[]{:S(2)}, u32[]{:S(2)}) %collective-permute-start.1) | collective-permute-done | bytes 65568 | tf_op jit(solution)/shard_map/ppermute | solution.py:493
  74.5 2.1 %content_first.1 = (f32[64,1024]{1,0:T(8,128)S(1)}, bf16[64,1024]{1,0:T(8,128)(2,1)S(1)}, bf16[128,2048]{1,0:T(8,128)(2,1)S(1)}) custom-call(f32[32,512]{1,0:T(8,128)S(1)} %embed_grads.1.mine_ref, f32[32,512]{1,0:T(8,128)S(1)} %collective-permute-done.1.other_ref, bf16[2048,512]{1,0:T(8,128)(2,1)S(1)} %get-tuple-element.41.we_ref, ...), custom_call_target="tpu_custom_call" | custom-call | tf_op jit(solution)/shard_map/content_first/pallas_call | solution.py:402
  76.6 1.5 %content_second.1 = (f32[64,1024]{1,0:T(8,128)S(1)}, bf16[64,1024]{1,0:T(8,128)(2,1)S(1)}) custom-call(bf16[128,2048]{1,0:T(8,128)(2,1)S(1)} %get-tuple-element.46.back_ref, bf16[2048,2048]{1,0:T(8,128)(2,1)S(1)} %get-tuple-element.43.wh_ref), custom_call_target="tpu_custom_call" | custom-call | tf_op jit(solution)/shard_map/content_second/pallas_call | solution.py:418
  78.2 0.2 collective-permute-start.2
  78.4 0.3 collective-permute-start.3
  78.7 0.8 %collective-permute-done.2.got1_ref = bf16[64,1024]{1,0:T(8,128)(2,1)S(1)} collective-permute-done((bf16[64,1024]{1,0:T(8,128)(2,1)S(1)}, bf16[64,1024]{1,0:T(8,128)(2,1)S(1)}, u32[]{:S(2)}, u32[]{:S(2)}) %collective-permute-start.2) | collective-permute-done | bytes 131104 | tf_op jit(solution)/shard_map/ppermute | solution.py:495
  79.6 0.2 collective-permute-done.3.got2_ref
  79.8 1.1 %combine.1 = bf16[32,2,2048]{2,1,0:T(2,128)(2,1)} custom-call(f32[64,1024]{1,0:T(8,128)S(1)} %get-tuple-element.44.keep1_ref, bf16[64,1024]{1,0:T(8,128)(2,1)S(1)} %collective-permute-done.2.got1_ref, f32[64,1024]{1,0:T(8,128)S(1)} %get-tuple-element.47.keep2_ref, bf16[64,1024]{1,0:T(8,128)(2,1)S(1)} %collective-permute-done.3.got2_ref), custom_call_target="tpu_custom_call" | custom-call | tf_op jit(solution)/shard_map/combine/pallas_call | solution.py:444
Async XLA Ops:
  0.0 7.5 %copy-start.2 = (bf16[256,512]{1,0:T(8,128)(2,1)S(1)}, bf16[256,512]{1,0:T(8,128)(2,1)}, u32[]{:S(2)}) copy-start(bf16[256,512]{1,0:T(8,128)(2,1)} %wp_ref.1) | copy-start | bytes 786436
  0.0 7.5 %copy-start.3 = (bf16[4,8,512]{2,1,0:T(8,128)(2,1)S(1)}, bf16[4,8,512]{2,1,0:T(8,128)(2,1)}, u32[]{:S(2)}) copy-start(bf16[4,8,512]{2,1,0:T(8,128)(2,1)} %param.19) | copy-start | bytes 98308
  6.9 2.3 %collective-permute-start = (f32[32,512]{1,0:T(8,128)S(1)}, f32[32,512]{1,0:T(8,128)S(1)}, u32[]{:S(2)}, u32[]{:S(2)}) collective-permute-start(f32[32,512]{1,0:T(8,128)S(1)} %get-tuple-element.27.after_ref.mine_ref), channel_id=1, source_target_pairs={{0,1},{1,0},{2,3},{3,2},{4,5},{5,4},{6,7},{7,6},{8,9},{9,8},{10,11... | collective-permute-start | bytes 196616 | tf_op jit(solution)/shard_map/ppermute | solution.py:480
  7.5 1.8 %copy-start = (bf16[512,256]{1,0:T(8,128)(2,1)S(1)}, bf16[512,256]{1,0:T(8,128)(2,1)}, u32[]{:S(2)}) copy-start(bf16[512,256]{1,0:T(8,128)(2,1)} %wq_ref.3) | copy-start | bytes 786436
  7.5 1.8 %copy-start.1 = (bf16[512,256]{1,0:T(8,128)(2,1)S(1)}, bf16[512,256]{1,0:T(8,128)(2,1)}, u32[]{:S(2)}) copy-start(bf16[512,256]{1,0:T(8,128)(2,1)} %wg_ref.3) | copy-start | bytes 786436
  7.5 20.2 %copy-start.4 = (s32[4,128]{1,0:T(4,128)S(1)}, s32[4,128]{1,0:T(4,128)}, u32[]{:S(2)}) copy-start(s32[4,128]{1,0:T(4,128)} %cutoff_ref.1) | copy-start | bytes 6148
  73.2 1.3 %collective-permute-start.1 = (f32[32,512]{1,0:T(8,128)S(1)}, f32[32,512]{1,0:T(8,128)S(1)}, u32[]{:S(2)}, u32[]{:S(2)}) collective-permute-start(f32[32,512]{1,0:T(8,128)S(1)} %embed_grads.1.mine_ref), channel_id=1, source_target_pairs={{0,1},{1,0},{2,3},{3,2},{4,5},{5,4},{6,7},{7,6},{8,9},{9,8},{10,11... | collective-permute-start | bytes 196616 | tf_op jit(solution)/shard_map/ppermute | solution.py:493
  78.2 1.4 %collective-permute-start.2 = (bf16[64,1024]{1,0:T(8,128)(2,1)S(1)}, bf16[64,1024]{1,0:T(8,128)(2,1)S(1)}, u32[]{:S(2)}, u32[]{:S(2)}) collective-permute-start(bf16[64,1024]{1,0:T(8,128)(2,1)S(1)} %get-tuple-element.45), channel_id=1, source_target_pairs={{0,1},{1,0},{2,3},{3,2},{4,5},{5,4},{6,7},{7,6},{8,9},{9,8},{10,11... | collective-permute-start | bytes 393224 | tf_op jit(solution)/shard_map/ppermute | solution.py:495
  78.4 1.4 %collective-permute-start.3 = (bf16[64,1024]{1,0:T(8,128)(2,1)S(1)}, bf16[64,1024]{1,0:T(8,128)(2,1)S(1)}, u32[]{:S(2)}, u32[]{:S(2)}) collective-permute-start(bf16[64,1024]{1,0:T(8,128)(2,1)S(1)} %get-tuple-element.48), channel_id=1, source_target_pairs={{0,1},{1,0},{2,3},{3,2},{4,5},{5,4},{6,7},{7,6},{8,9},{9,8},{10,11... | collective-permute-start | bytes 393224 | tf_op jit(solution)/shard_map/ppermute | solution.py:497

commit v4 on v3

--- a/solution.py
+++ b/solution.py
@@ -105,7 +105,7 @@
     hidden = w_hidden.shape[1]
     model = w_embed.shape[1]
     return pl.pallas_call(
-        functools.partial(encode_kernel, parts, block, 3),
+        functools.partial(encode_kernel, parts, block, 8),
         in_specs=[pl.BlockSpec(memory_space=pltpu.HBM)] * 3,
         out_specs=in_vmem(4),
         out_shape=[
@@ -180,7 +180,6 @@
 def forward_kernel(
     heads,
     block,
-    group,
     query_ref,
     cutoff_ref,
     first_key_ref,
@@ -203,8 +202,9 @@
             pltpu.make_async_copy(value_hbm.at[user], value_ref.at[user - 1], sems.at[1, user - 1]),
         )
 
-    for user in range(1, min(3, users)):
-        for copy in fetch(user):
+    copies = {user: fetch(user) for user in range(1, users)}
+    for user in range(1, users):
+        for copy in copies[user]:
             copy.start()
     targets, local = query_ref.shape[0] * query_ref.shape[2], query_ref.shape[3]
     one = jnp.asarray(1.0, BF16)
@@ -218,31 +218,25 @@
         if user == 0:
             keys_here, values_here = first_key_ref, first_value_ref
         else:
-            if user + 2 < users:
-                for copy in fetch(user + 2):
-                    copy.start()
-            for copy in fetch(user):
-                copy.wait()
+            copies[user][0].wait()
             keys_here, values_here = key_ref.at[user - 1], value_ref.at[user - 1]
-        totals = [jnp.zeros((targets, DH), F32) for _ in range(heads)]
-        for first in range(0, events, block * group):
-            span = slice(first, first + block * group)
-            for head in range(heads):
-                lanes = slice(head * DH, (head + 1) * DH)
-                weights = []
-                for start in range(first, first + block * group, block):
-                    rows = slice(start, start + block)
-                    left = (limit_ref[...] - float(start)).astype(BF16)
-                    visible = spots < left
-                    half = contract_last(queries[:, lanes], keys_here[rows, lanes]).astype(BF16)
-                    tanh = jnp.where(visible, jnp.tanh(half), -one)
-                    lift = one + tanh
-                    weight = half * lift
-                    slope_ref[user, head, :, rows] = lift + weight * (one - tanh)
-                    weights.append(weight)
-                totals[head] = totals[head] + matmul(
-                    jnp.concatenate(weights, axis=-1), values_here[span, lanes]
-                )
+        totals = []
+        for head in range(heads):
+            lanes = slice(head * DH, (head + 1) * DH)
+            weights = []
+            for start in range(0, events, block):
+                rows = slice(start, start + block)
+                left = (limit_ref[...] - float(start)).astype(BF16)
+                visible = spots < left
+                half = contract_last(queries[:, lanes], keys_here[rows, lanes]).astype(BF16)
+                tanh = jnp.where(visible, jnp.tanh(half), -one)
+                lift = one + tanh
+                weight = half * lift
+                slope_ref[user, head, :, rows] = lift + weight * (one - tanh)
+                weights.append(weight)
+            if user > 0 and head == 0:
+                copies[user][1].wait()
+            totals.append(matmul(jnp.concatenate(weights, axis=-1), values_here[:, lanes]))
         total = jnp.concatenate(totals, axis=-1)
         out_ref[:, pl.ds(user, 1)] = total.reshape(-1, 1, query_ref.shape[2], local).astype(BF16)
 
@@ -252,7 +246,7 @@
     events = keys.shape[1]
     targets = copies * rows
     return pl.pallas_call(
-        functools.partial(forward_kernel, heads, *chunks_of(events)),
+        functools.partial(forward_kernel, heads, chunks_of(events)[0]),
         in_specs=in_vmem(4) + [pl.BlockSpec(memory_space=pltpu.HBM)] * 2,
         out_specs=in_vmem(4),
         out_shape=[
@@ -428,27 +422,52 @@
     )(kept_in_vmem(back), kept_in_vmem(w_hidden))
 
 
-def combine_kernel(keep1_ref, got1_ref, keep2_ref, got2_ref, out_ref):
-    count, half, width = out_ref.shape
+def placed_rows(keep_ref, got_ref, count, half):
     rows = count * half
     spot = lax.broadcasted_iota(jnp.int32, (rows, rows), 0)
     from_row = lax.broadcasted_iota(jnp.int32, (rows, rows), 1)
     order = jnp.where(from_row == (spot % half) * count + spot // half, 1.0, 0.0).astype(BF16)
-    for first, keep_ref, got_ref in ((0, keep1_ref, got1_ref), (width // 2, keep2_ref, got2_ref)):
-        total = (keep_ref[...] + got_ref[...].astype(F32)).astype(BF16)
-        placed = matmul(order, total).reshape(count, half, width // 2)
-        out_ref[:, :, first : first + width // 2] = placed.astype(BF16)
-
-
-def combine(pieces, count, half, width):
-    return pl.pallas_call(
-        combine_kernel,
-        in_specs=in_vmem(4),
+    total = (keep_ref[...] + got_ref[...].astype(F32)).astype(BF16)
+    return matmul(order, total).reshape(count, half, -1).astype(BF16)
+
+
+def place_kernel(keep_ref, got_ref, out_ref):
+    out_ref[...] = placed_rows(keep_ref, got_ref, *out_ref.shape[:2])
+
+
+def place(keep, got, count, half):
+    return pl.pallas_call(
+        place_kernel,
+        in_specs=in_vmem(2),
         out_specs=in_vmem(1)[0],
-        out_shape=jax.ShapeDtypeStruct((count, half, width), BF16),
+        out_shape=pltpu.VMEM((count, half, keep.shape[1]), BF16),
         compiler_params=params(8),
-        name="combine",
-    )(*pieces)
+        name="place",
+    )(keep, got)
+
+
+def finish_kernel(first_ref, keep_ref, got_ref, out_hbm, last_ref, sems):
+    width = first_ref.shape[2]
+    early = pltpu.make_async_copy(first_ref, out_hbm.at[:, :, pl.ds(0, width)], sems.at[0])
+    early.start()
+    last_ref[...] = placed_rows(keep_ref, got_ref, *first_ref.shape[:2])
+    late = pltpu.make_async_copy(last_ref, out_hbm.at[:, :, pl.ds(width, width)], sems.at[1])
+    late.start()
+    early.wait()
+    late.wait()
+
+
+def finish(first, keep, got):
+    count, half, width = first.shape
+    return pl.pallas_call(
+        finish_kernel,
+        in_specs=in_vmem(3),
+        out_specs=pl.BlockSpec(memory_space=pltpu.HBM),
+        out_shape=jax.ShapeDtypeStruct((count, half, 2 * width), BF16),
+        scratch_shapes=[pltpu.VMEM(first.shape, BF16), pltpu.SemaphoreType.DMA((2,))],
+        compiler_params=params(8),
+        name="finish",
+    )(kept_in_vmem(first), keep, got)
 
 
 def body(
@@ -494,9 +513,10 @@
     keep1, send1, back = content_first(mine, other, w_embed, hidden_slope, w_hidden, parts, 256)
     got1 = lax.ppermute(send1, "head", swap)
     keep2, send2 = content_second(back, w_hidden, 256)
+    half = parts // head_count
     got2 = lax.ppermute(send2, "head", swap)
-    half = parts // head_count
-    total = combine((keep1, got1, keep2, got2), count, half, width)
+    first = place(keep1, got1, count, half)
+    total = finish(first, keep2, got2)
     return total.reshape(users, shard_rows, half, width)
 
 

time: 81.2 us -> 83.3 us (1.026)
  Pallas kernels: 21.1 us -> 23.4 us
    pallas_call x3 -> x4, Pallas kernels: 12.4 us -> 14.6 us  [the longest x1 8.9 us: encode(): pl.pallas_call(functools.partial(encode_kernel, parts, block, 8), in_spec...]
    ppermute x1, waiting for transfers between devices: 0.84 us -> 0.01 us  [body(): got1 = lax.ppermute(send1, 'head', swap)]
  transfers between devices with their start and end apart: 4 -> 4, of which waited for: 3 -> 2; matrix products, arithmetic and copies ran while one was open for 0% -> 0% of each run, Pallas kernels for 2% -> 4%
where the time goes in v4:
time: 83.3 us; the launch traced here: 83 us
  blocking collectives  56.2 us (67%)
  Pallas kernels  23.4 us (28%)
  waiting for transfers between devices  1.98 us (2%)
  starting transfers between devices  1.2 us (1%)
    all_to_all x4, blocking collectives, to_owner(): return lax.all_to_all(blocks, 'ctx', 0, 0, tiled=True)  56.2 us
    pallas_call x1, Pallas kernels, encode(): pl.pallas_call(functools.partial(encode_kernel, parts, block, 8), in_spec...  8.9 us
    pallas_call x1, Pallas kernels, forward_attention(): pl.pallas_call(functools.partial(forward_kernel, heads, chunks_of(events)...  4.53 us
    pallas_call x1, Pallas kernels, backward_attention(): pl.pallas_call(functools.partial(backward_kernel, DH ** (-0.5), heads, *c...  2.67 us
    pallas_call x1, Pallas kernels, content_first(): pl.pallas_call(functools.partial(content_first_kernel, parts, block), in_...  2.13 us
    pallas_call x1, Pallas kernels, warm(): pl.pallas_call(warm_kernel, in_specs=in_vmem(3) + [pl.BlockSpec(memory_sp...  1.71 us
  transfers between devices with their start and end apart: 4, of which 2 were waited for; matrix products, arithmetic and copies ran while one was open for 0% of the time, Pallas kernels for 4%

profile of v4, /device:TPU:0, one launch (start us, length us, event | category | flops | bytes accessed | tf_op | source)
XLA Modules:
  0.0 83.0 jit_solution(8761702318535000891)
XLA Ops:
  0.0 0.0 copy-start.2
  0.0 0.0 copy-start.3
  0.0 8.9 %encode.1 = (f32[128,2048]{1,0:T(8,128)S(1)}, f32[32,512]{1,0:T(8,128)S(1)}, bf16[2048,2048]{1,0:T(8,128)(2,1)S(1)}, bf16[2048,512]{1,0:T(8,128)(2,1)S(1)}) custom-call(bf16[32,4,2048]{2,1,0:T(4,128)(2,1)} %bitcast.4, bf16[2048,2048]{1,0:T(8,128)(2,1)} %wh_hbm.1, bf16[2048,512]{1,0:T(8,128)(2,1)} %we_hbm.1), custom_call_target="tpu_custom_call" | custom-call | tf_op jit(solution)/shard_map/encode/pallas_call | solution.py:107
  8.9 0.6 collective-permute-start
  9.5 0.0 copy-done.2
  9.5 0.0 copy-done.3
  9.5 0.0 copy-start
  9.5 0.0 copy-start.4
  9.5 1.7 %warm.1 = (f32[32,256]{1,0:T(8,128)S(1)}, bf16[2304,256]{1,0:T(8,128)(2,1)S(1)}, bf16[2304,256]{1,0:T(8,128)(2,1)S(1)}) custom-call(f32[32,512]{1,0:T(8,128)S(1)} %get-tuple-element.27.after_ref.mine_ref, bf16[32,512]{1,0:T(8,128)(2,1)S(1)} %bitcast.3, bf16[256,512]{1,0:T(8,128)(2,1)S(1)} %copy-done.2, bf16[4,2304,256]{2,1,0:T(8,128)(2,1)} %key_hbm.3, ...), custom_call_target="tpu_custom_call" | custom-call | tf_op jit(solution)/shard_map/warm/pallas_call | solution.py:141
  11.2 0.0 collective-permute-done.other_ref
  11.2 0.0 copy-done
  11.2 0.0 copy-done.1
  11.2 0.2 project.1
  11.5 18.2 %all_to_all.20.query_ref = bf16[16,4,8,256]{3,2,1,0:T(8,128)(2,1)S(1)} all-to-all(bf16[16,4,8,256]{3,2,1,0:T(8,128)(2,1)S(1)} %get-tuple-element.29), channel_id=1, replica_groups=mesh['ctx'=16,'head'=2] {'ctx'}, dimensions={0} | all-to-all | bytes 524288 | tf_op jit(solution)/shard_map/all_to_all | solution.py:494
  29.7 0.0 copy-done.4
  29.7 4.5 %attention_forward.1 = (bf16[16,4,8,256]{3,2,1,0:T(8,128)(2,1)S(1)}, bf16[4,2,128,2304]{3,2,1,0:T(8,128)(2,1)S(1)}, bf16[3,2304,256]{2,1,0:T(8,128)(2,1)S(1)}, bf16[3,2304,256]{2,1,0:T(8,128)(2,1)S(1)}) custom-call(bf16[16,4,8,256]{3,2,1,0:T(8,128)(2,1)S(1)} %all_to_all.20.query_ref, s32[4,128]{1,0:T(4,128)S(1)} %copy-done.4, ...), custom_call_target="tpu_custom_call" | custom-call | tf_op jit(solution)/shard_map/attention_forward/pallas_call | solution.py:248
  34.2 12.8 %all_to_all.21.parts_ref = bf16[16,4,8,256]{3,2,1,0:T(8,128)(2,1)S(1)} all-to-all(bf16[16,4,8,256]{3,2,1,0:T(8,128)(2,1)S(1)} %get-tuple-element.32), channel_id=1, replica_groups=mesh['ctx'=16,'head'=2] {'ctx'}, dimensions={0} | all-to-all | bytes 524288 | tf_op jit(solution)/shard_map/all_to_all | solution.py:494
  47.1 0.2 norm_grads.1
  47.3 12.6 %all_to_all.22.grad_ref = bf16[16,4,8,256]{3,2,1,0:T(8,128)(2,1)S(1)} all-to-all(bf16[16,4,8,256]{3,2,1,0:T(8,128)(2,1)S(1)} %get-tuple-element.34), channel_id=1, replica_groups=mesh['ctx'=16,'head'=2] {'ctx'}, dimensions={0} | all-to-all | bytes 524288 | tf_op jit(solution)/shard_map/all_to_all | solution.py:494
  59.9 2.7 %attention_backward.1 = bf16[16,4,8,256]{3,2,1,0:T(8,128)(2,1)S(1)} custom-call(bf16[16,4,8,256]{3,2,1,0:T(8,128)(2,1)S(1)} %all_to_all.22.grad_ref, bf16[4,2,128,2304]{3,2,1,0:T(8,128)(2,1)S(1)} %get-tuple-element.35.slope_ref, bf16[2304,256]{1,0:T(8,128)(2,1)S(1)} %get-tuple-element.30.first_key_ref, ...), custom_call_target="tpu_custom_call" | custom-call | tf_op jit(solution)/shard_map/attention_backward/pallas_call | solution.py:337
  62.6 12.5 %all_to_all.23.parts_ref = bf16[16,4,8,256]{3,2,1,0:T(8,128)(2,1)S(1)} all-to-all(bf16[16,4,8,256]{3,2,1,0:T(8,128)(2,1)S(1)} %attention_backward.1), channel_id=1, replica_groups=mesh['ctx'=16,'head'=2] {'ctx'}, dimensions={0} | all-to-all | bytes 524288 | tf_op jit(solution)/shard_map/all_to_all | solution.py:494
  75.1 0.3 embed_grads.1.mine_ref
  75.4 0.0 collective-permute-start.1
  75.4 1.3 %collective-permute-done.1.other_ref = f32[32,512]{1,0:T(8,128)S(1)} collective-permute-done((f32[32,512]{1,0:T(8,128)S(1)}, f32[32,512]{1,0:T(8,128)S(1)}, u32[]{:S(2)}, u32[]{:S(2)}) %collective-permute-start.1) | collective-permute-done | bytes 65568 | tf_op jit(solution)/shard_map/ppermute | solution.py:512
  76.6 2.1 %content_first.1 = (f32[64,1024]{1,0:T(8,128)S(1)}, bf16[64,1024]{1,0:T(8,128)(2,1)S(1)}, bf16[128,2048]{1,0:T(8,128)(2,1)S(1)}) custom-call(f32[32,512]{1,0:T(8,128)S(1)} %embed_grads.1.mine_ref, f32[32,512]{1,0:T(8,128)S(1)} %collective-permute-done.1.other_ref, bf16[2048,512]{1,0:T(8,128)(2,1)S(1)} %get-tuple-element.41.we_ref, ...), custom_call_target="tpu_custom_call" | custom-call | tf_op jit(solution)/shard_map/content_first/pallas_call | solution.py:396
  78.8 0.2 collective-permute-start.2
  79.0 1.5 %content_second.1 = (f32[64,1024]{1,0:T(8,128)S(1)}, bf16[64,1024]{1,0:T(8,128)(2,1)S(1)}) custom-call(bf16[128,2048]{1,0:T(8,128)(2,1)S(1)} %get-tuple-element.46.back_ref, bf16[2048,2048]{1,0:T(8,128)(2,1)S(1)} %get-tuple-element.43.wh_ref), custom_call_target="tpu_custom_call" | custom-call | tf_op jit(solution)/shard_map/content_second/pallas_call | solution.py:412
  80.5 0.4 collective-permute-start.3
  80.9 0.0 collective-permute-done.2.got_ref
  80.9 0.3 place.1.first_ref
  81.2 0.7 collective-permute-done.3.got_ref
  81.9 0.9 %finish.1 = bf16[32,2,2048]{2,1,0:T(2,128)(2,1)} custom-call(bf16[32,2,1024]{2,1,0:T(2,128)(2,1)S(1)} %place.1.first_ref, f32[64,1024]{1,0:T(8,128)S(1)} %get-tuple-element.47.keep_ref, bf16[64,1024]{1,0:T(8,128)(2,1)S(1)} %collective-permute-done.3.got_ref), custom_call_target="tpu_custom_call" | custom-call | tf_op jit(solution)/shard_map/finish/pallas_call | solution.py:462
  (1 shorter events, 0.0 us)
Async XLA Ops:
  0.0 9.5 %copy-start.2 = (bf16[256,512]{1,0:T(8,128)(2,1)S(1)}, bf16[256,512]{1,0:T(8,128)(2,1)}, u32[]{:S(2)}) copy-start(bf16[256,512]{1,0:T(8,128)(2,1)} %wp_ref.1) | copy-start | bytes 786436
  0.0 9.5 %copy-start.3 = (bf16[4,8,512]{2,1,0:T(8,128)(2,1)S(1)}, bf16[4,8,512]{2,1,0:T(8,128)(2,1)}, u32[]{:S(2)}) copy-start(bf16[4,8,512]{2,1,0:T(8,128)(2,1)} %param.19) | copy-start | bytes 98308
  8.9 2.3 %collective-permute-start = (f32[32,512]{1,0:T(8,128)S(1)}, f32[32,512]{1,0:T(8,128)S(1)}, u32[]{:S(2)}, u32[]{:S(2)}) collective-permute-start(f32[32,512]{1,0:T(8,128)S(1)} %get-tuple-element.27.after_ref.mine_ref), channel_id=1, source_target_pairs={{0,1},{1,0},{2,3},{3,2},{4,5},{5,4},{6,7},{7,6},{8,9},{9,8},{10,11... | collective-permute-start | bytes 196616 | tf_op jit(solution)/shard_map/ppermute | solution.py:499
  9.5 1.8 %copy-start = (bf16[512,256]{1,0:T(8,128)(2,1)S(1)}, bf16[512,256]{1,0:T(8,128)(2,1)}, u32[]{:S(2)}) copy-start(bf16[512,256]{1,0:T(8,128)(2,1)} %wq_ref.3) | copy-start | bytes 786436
  9.5 1.8 %copy-start.1 = (bf16[512,256]{1,0:T(8,128)(2,1)S(1)}, bf16[512,256]{1,0:T(8,128)(2,1)}, u32[]{:S(2)}) copy-start(bf16[512,256]{1,0:T(8,128)(2,1)} %wg_ref.3) | copy-start | bytes 786436
  9.5 20.2 %copy-start.4 = (s32[4,128]{1,0:T(4,128)S(1)}, s32[4,128]{1,0:T(4,128)}, u32[]{:S(2)}) copy-start(s32[4,128]{1,0:T(4,128)} %cutoff_ref.1) | copy-start | bytes 6148
  75.4 1.3 %collective-permute-start.1 = (f32[32,512]{1,0:T(8,128)S(1)}, f32[32,512]{1,0:T(8,128)S(1)}, u32[]{:S(2)}, u32[]{:S(2)}) collective-permute-start(f32[32,512]{1,0:T(8,128)S(1)} %embed_grads.1.mine_ref), channel_id=1, source_target_pairs={{0,1},{1,0},{2,3},{3,2},{4,5},{5,4},{6,7},{7,6},{8,9},{9,8},{10,11... | collective-permute-start | bytes 196616 | tf_op jit(solution)/shard_map/ppermute | solution.py:512
  78.8 2.2 %collective-permute-start.2 = (bf16[64,1024]{1,0:T(8,128)(2,1)S(1)}, bf16[64,1024]{1,0:T(8,128)(2,1)S(1)}, u32[]{:S(2)}, u32[]{:S(2)}) collective-permute-start(bf16[64,1024]{1,0:T(8,128)(2,1)S(1)} %get-tuple-element.45), channel_id=1, source_target_pairs={{0,1},{1,0},{2,3},{3,2},{4,5},{5,4},{6,7},{7,6},{8,9},{9,8},{10,11... | collective-permute-start | bytes 393224 | tf_op jit(solution)/shard_map/ppermute | solution.py:514
  80.5 1.4 %collective-permute-start.3 = (bf16[64,1024]{1,0:T(8,128)(2,1)S(1)}, bf16[64,1024]{1,0:T(8,128)(2,1)S(1)}, u32[]{:S(2)}, u32[]{:S(2)}) collective-permute-start(bf16[64,1024]{1,0:T(8,128)(2,1)S(1)} %get-tuple-element.48), channel_id=1, source_target_pairs={{0,1},{1,0},{2,3},{3,2},{4,5},{5,4},{6,7},{7,6},{8,9},{9,8},{10,11... | collective-permute-start | bytes 393224 | tf_op jit(solution)/shard_map/ppermute | solution.py:517

commit v5 on v3

--- a/solution.py
+++ b/solution.py
@@ -72,14 +72,16 @@
         )
     rows_copy = pltpu.make_async_copy(rows_hbm, rows_ref, row_sem)
     rows_copy.start()
-    for pair in copies[:depth]:
-        pair[0].start()
-        pair[1].start()
+    copies[0][0].start()
     spot = lax.broadcasted_iota(jnp.int32, (total_rows, total_rows), 0)
     from_row = lax.broadcasted_iota(jnp.int32, (total_rows, total_rows), 1)
     wanted = (spot % count) * parts + spot // count
     order = jnp.where(from_row == wanted, 1.0, 0.0).astype(BF16)
     rows_copy.wait()
+    copies[0][1].start()
+    for pair in copies[1:depth]:
+        pair[0].start()
+        pair[1].start()
     rows = rows_ref[...].astype(F32).reshape(total_rows, rows_ref.shape[2]).astype(BF16)
     rm_ref[...] = matmul(order, rows).astype(BF16)
     total = jnp.zeros((total_rows, we_ref.shape[1]), F32)
@@ -105,7 +107,7 @@
     hidden = w_hidden.shape[1]
     model = w_embed.shape[1]
     return pl.pallas_call(
-        functools.partial(encode_kernel, parts, block, 3),
+        functools.partial(encode_kernel, parts, block, 4),
         in_specs=[pl.BlockSpec(memory_space=pltpu.HBM)] * 3,
         out_specs=in_vmem(4),
         out_shape=[
@@ -428,27 +430,52 @@
     )(kept_in_vmem(back), kept_in_vmem(w_hidden))
 
 
-def combine_kernel(keep1_ref, got1_ref, keep2_ref, got2_ref, out_ref):
-    count, half, width = out_ref.shape
+def placed_rows(keep_ref, got_ref, count, half):
     rows = count * half
     spot = lax.broadcasted_iota(jnp.int32, (rows, rows), 0)
     from_row = lax.broadcasted_iota(jnp.int32, (rows, rows), 1)
     order = jnp.where(from_row == (spot % half) * count + spot // half, 1.0, 0.0).astype(BF16)
-    for first, keep_ref, got_ref in ((0, keep1_ref, got1_ref), (width // 2, keep2_ref, got2_ref)):
-        total = (keep_ref[...] + got_ref[...].astype(F32)).astype(BF16)
-        placed = matmul(order, total).reshape(count, half, width // 2)
-        out_ref[:, :, first : first + width // 2] = placed.astype(BF16)
-
-
-def combine(pieces, count, half, width):
-    return pl.pallas_call(
-        combine_kernel,
-        in_specs=in_vmem(4),
+    total = (keep_ref[...] + got_ref[...].astype(F32)).astype(BF16)
+    return matmul(order, total).reshape(count, half, -1).astype(BF16)
+
+
+def place_kernel(keep_ref, got_ref, out_ref):
+    out_ref[...] = placed_rows(keep_ref, got_ref, *out_ref.shape[:2])
+
+
+def place(keep, got, count, half):
+    return pl.pallas_call(
+        place_kernel,
+        in_specs=in_vmem(2),
         out_specs=in_vmem(1)[0],
-        out_shape=jax.ShapeDtypeStruct((count, half, width), BF16),
+        out_shape=pltpu.VMEM((count, half, keep.shape[1]), BF16),
         compiler_params=params(8),
-        name="combine",
-    )(*pieces)
+        name="place",
+    )(keep, got)
+
+
+def finish_kernel(first_ref, keep_ref, got_ref, out_hbm, last_ref, sems):
+    width = first_ref.shape[2]
+    early = pltpu.make_async_copy(first_ref, out_hbm.at[:, :, pl.ds(0, width)], sems.at[0])
+    early.start()
+    last_ref[...] = placed_rows(keep_ref, got_ref, *first_ref.shape[:2])
+    late = pltpu.make_async_copy(last_ref, out_hbm.at[:, :, pl.ds(width, width)], sems.at[1])
+    late.start()
+    early.wait()
+    late.wait()
+
+
+def finish(first, keep, got):
+    count, half, width = first.shape
+    return pl.pallas_call(
+        finish_kernel,
+        in_specs=in_vmem(3),
+        out_specs=pl.BlockSpec(memory_space=pltpu.HBM),
+        out_shape=jax.ShapeDtypeStruct((count, half, 2 * width), BF16),
+        scratch_shapes=[pltpu.VMEM(first.shape, BF16), pltpu.SemaphoreType.DMA((2,))],
+        compiler_params=params(8),
+        name="finish",
+    )(kept_in_vmem(first), keep, got)
 
 
 def body(
@@ -475,7 +502,7 @@
         return lax.all_to_all(blocks, "ctx", 0, 0, tiled=True)
 
     hidden_slope, mine, w_hidden, w_embed = encode(
-        content_rows.reshape(count, parts, width), w_hidden, w_embed, 256
+        content_rows.reshape(count, parts, width), w_hidden, w_embed, 512
     )
     other = lax.ppermute(mine, "head", swap)
     cotangent = out_cotangent.reshape(count, -1)
@@ -494,9 +521,10 @@
     keep1, send1, back = content_first(mine, other, w_embed, hidden_slope, w_hidden, parts, 256)
     got1 = lax.ppermute(send1, "head", swap)
     keep2, send2 = content_second(back, w_hidden, 256)
+    half = parts // head_count
     got2 = lax.ppermute(send2, "head", swap)
-    half = parts // head_count
-    total = combine((keep1, got1, keep2, got2), count, half, width)
+    first = place(keep1, got1, count, half)
+    total = finish(first, keep2, got2)
     return total.reshape(users, shard_rows, half, width)
 
 

time: 81.2 us -> 79.7 us (0.982)
  Pallas kernels: 21.1 us -> 19.7 us
    pallas_call x2 -> x3, Pallas kernels: 8.02 us -> 6.61 us  [the longest x1 5.39 us: encode(): pl.pallas_call(functools.partial(encode_kernel, parts, block, 4), in_spec...]
    ppermute x1, waiting for transfers between devices: 0.84 us -> 0.01 us  [body(): got1 = lax.ppermute(send1, 'head', swap)]
  transfers between devices with their start and end apart: 4 -> 4, of which waited for: 3 -> 2; matrix products, arithmetic and copies ran while one was open for 0% -> 0% of each run, Pallas kernels for 2% -> 4%
where the time goes in v5:
time: 79.7 us; the launch traced here: 79.4 us
  blocking collectives  56.2 us (71%)
  Pallas kernels  19.7 us (25%)
  waiting for transfers between devices  1.98 us (2%)
  starting transfers between devices  1.2 us (2%)
    all_to_all x4, blocking collectives, to_owner(): return lax.all_to_all(blocks, 'ctx', 0, 0, tiled=True)  56.2 us
    pallas_call x1, Pallas kernels, encode(): pl.pallas_call(functools.partial(encode_kernel, parts, block, 4), in_spec...  5.39 us
    pallas_call x1, Pallas kernels, forward_attention(): pl.pallas_call(functools.partial(forward_kernel, heads, *chunks_of(events...  4.37 us
    pallas_call x1, Pallas kernels, backward_attention(): pl.pallas_call(functools.partial(backward_kernel, DH ** (-0.5), heads, *c...  2.67 us
    pallas_call x1, Pallas kernels, content_first(): pl.pallas_call(functools.partial(content_first_kernel, parts, block), in_...  2.14 us
    pallas_call x1, Pallas kernels, warm(): pl.pallas_call(warm_kernel, in_specs=in_vmem(3) + [pl.BlockSpec(memory_sp...  1.71 us
  transfers between devices with their start and end apart: 4, of which 2 were waited for; matrix products, arithmetic and copies ran while one was open for 0% of the time, Pallas kernels for 4%

profile of v5, /device:TPU:0, one launch (start us, length us, event | category | flops | bytes accessed | tf_op | source)
XLA Modules:
  0.0 79.4 jit_solution(8260066071219126388)
XLA Ops:
  0.0 0.0 copy-start.2
  0.0 0.0 copy-start.3
  0.0 5.4 %encode.1 = (f32[128,2048]{1,0:T(8,128)S(1)}, f32[32,512]{1,0:T(8,128)S(1)}, bf16[2048,2048]{1,0:T(8,128)(2,1)S(1)}, bf16[2048,512]{1,0:T(8,128)(2,1)S(1)}) custom-call(bf16[32,4,2048]{2,1,0:T(4,128)(2,1)} %bitcast.4, bf16[2048,2048]{1,0:T(8,128)(2,1)} %wh_hbm.1, bf16[2048,512]{1,0:T(8,128)(2,1)} %we_hbm.1), custom_call_target="tpu_custom_call" | custom-call | tf_op jit(solution)/shard_map/encode/pallas_call | solution.py:109
  5.4 0.6 collective-permute-start
  6.0 0.0 copy-done.2
  6.0 0.0 copy-done.3
  6.0 0.0 copy-start
  6.0 0.0 copy-start.4
  6.0 1.7 %warm.1 = (f32[32,256]{1,0:T(8,128)S(1)}, bf16[2304,256]{1,0:T(8,128)(2,1)S(1)}, bf16[2304,256]{1,0:T(8,128)(2,1)S(1)}) custom-call(f32[32,512]{1,0:T(8,128)S(1)} %get-tuple-element.27.after_ref.mine_ref, bf16[32,512]{1,0:T(8,128)(2,1)S(1)} %bitcast.3, bf16[256,512]{1,0:T(8,128)(2,1)S(1)} %copy-done.2, bf16[4,2304,256]{2,1,0:T(8,128)(2,1)} %key_hbm.3, ...), custom_call_target="tpu_custom_call" | custom-call | tf_op jit(solution)/shard_map/warm/pallas_call | solution.py:143
  7.7 0.0 collective-permute-done.other_ref
  7.7 0.0 copy-done
  7.7 0.0 copy-done.1
  7.7 0.2 project.1
  8.0 18.2 %all_to_all.20.query_ref = bf16[16,4,8,256]{3,2,1,0:T(8,128)(2,1)S(1)} all-to-all(bf16[16,4,8,256]{3,2,1,0:T(8,128)(2,1)S(1)} %get-tuple-element.29), channel_id=1, replica_groups=mesh['ctx'=16,'head'=2] {'ctx'}, dimensions={0} | all-to-all | bytes 524288 | tf_op jit(solution)/shard_map/all_to_all | solution.py:502
  26.2 0.0 copy-done.4
  26.2 4.4 %attention_forward.1 = (bf16[16,4,8,256]{3,2,1,0:T(8,128)(2,1)S(1)}, bf16[4,2,128,2304]{3,2,1,0:T(8,128)(2,1)S(1)}, bf16[3,2304,256]{2,1,0:T(8,128)(2,1)S(1)}, bf16[3,2304,256]{2,1,0:T(8,128)(2,1)S(1)}) custom-call(bf16[16,4,8,256]{3,2,1,0:T(8,128)(2,1)S(1)} %all_to_all.20.query_ref, s32[4,128]{1,0:T(4,128)S(1)} %copy-done.4, ...), custom_call_target="tpu_custom_call" | custom-call | tf_op jit(solution)/shard_map/attention_forward/pallas_call | solution.py:256
  30.5 12.8 %all_to_all.21.parts_ref = bf16[16,4,8,256]{3,2,1,0:T(8,128)(2,1)S(1)} all-to-all(bf16[16,4,8,256]{3,2,1,0:T(8,128)(2,1)S(1)} %get-tuple-element.32), channel_id=1, replica_groups=mesh['ctx'=16,'head'=2] {'ctx'}, dimensions={0} | all-to-all | bytes 524288 | tf_op jit(solution)/shard_map/all_to_all | solution.py:502
  43.4 0.2 norm_grads.1
  43.6 12.6 %all_to_all.22.grad_ref = bf16[16,4,8,256]{3,2,1,0:T(8,128)(2,1)S(1)} all-to-all(bf16[16,4,8,256]{3,2,1,0:T(8,128)(2,1)S(1)} %get-tuple-element.34), channel_id=1, replica_groups=mesh['ctx'=16,'head'=2] {'ctx'}, dimensions={0} | all-to-all | bytes 524288 | tf_op jit(solution)/shard_map/all_to_all | solution.py:502
  56.2 2.7 %attention_backward.1 = bf16[16,4,8,256]{3,2,1,0:T(8,128)(2,1)S(1)} custom-call(bf16[16,4,8,256]{3,2,1,0:T(8,128)(2,1)S(1)} %all_to_all.22.grad_ref, bf16[4,2,128,2304]{3,2,1,0:T(8,128)(2,1)S(1)} %get-tuple-element.35.slope_ref, bf16[2304,256]{1,0:T(8,128)(2,1)S(1)} %get-tuple-element.30.first_key_ref, ...), custom_call_target="tpu_custom_call" | custom-call | tf_op jit(solution)/shard_map/attention_backward/pallas_call | solution.py:345
  58.9 12.5 %all_to_all.23.parts_ref = bf16[16,4,8,256]{3,2,1,0:T(8,128)(2,1)S(1)} all-to-all(bf16[16,4,8,256]{3,2,1,0:T(8,128)(2,1)S(1)} %attention_backward.1), channel_id=1, replica_groups=mesh['ctx'=16,'head'=2] {'ctx'}, dimensions={0} | all-to-all | bytes 524288 | tf_op jit(solution)/shard_map/all_to_all | solution.py:502
  71.4 0.3 embed_grads.1.mine_ref
  71.7 0.0 collective-permute-start.1
  71.7 1.3 %collective-permute-done.1.other_ref = f32[32,512]{1,0:T(8,128)S(1)} collective-permute-done((f32[32,512]{1,0:T(8,128)S(1)}, f32[32,512]{1,0:T(8,128)S(1)}, u32[]{:S(2)}, u32[]{:S(2)}) %collective-permute-start.1) | collective-permute-done | bytes 65568 | tf_op jit(solution)/shard_map/ppermute | solution.py:520
  73.0 2.1 %content_first.1 = (f32[64,1024]{1,0:T(8,128)S(1)}, bf16[64,1024]{1,0:T(8,128)(2,1)S(1)}, bf16[128,2048]{1,0:T(8,128)(2,1)S(1)}) custom-call(f32[32,512]{1,0:T(8,128)S(1)} %embed_grads.1.mine_ref, f32[32,512]{1,0:T(8,128)S(1)} %collective-permute-done.1.other_ref, bf16[2048,512]{1,0:T(8,128)(2,1)S(1)} %get-tuple-element.41.we_ref, ...), custom_call_target="tpu_custom_call" | custom-call | tf_op jit(solution)/shard_map/content_first/pallas_call | solution.py:404
  75.1 0.2 collective-permute-start.2
  75.3 1.5 %content_second.1 = (f32[64,1024]{1,0:T(8,128)S(1)}, bf16[64,1024]{1,0:T(8,128)(2,1)S(1)}) custom-call(bf16[128,2048]{1,0:T(8,128)(2,1)S(1)} %get-tuple-element.46.back_ref, bf16[2048,2048]{1,0:T(8,128)(2,1)S(1)} %get-tuple-element.43.wh_ref), custom_call_target="tpu_custom_call" | custom-call | tf_op jit(solution)/shard_map/content_second/pallas_call | solution.py:420
  76.9 0.4 collective-permute-start.3
  77.3 0.0 collective-permute-done.2.got_ref
  77.3 0.3 place.1.first_ref
  77.6 0.7 collective-permute-done.3.got_ref
  78.3 0.9 %finish.1 = bf16[32,2,2048]{2,1,0:T(2,128)(2,1)} custom-call(bf16[32,2,1024]{2,1,0:T(2,128)(2,1)S(1)} %place.1.first_ref, f32[64,1024]{1,0:T(8,128)S(1)} %get-tuple-element.47.keep_ref, bf16[64,1024]{1,0:T(8,128)(2,1)S(1)} %collective-permute-done.3.got_ref), custom_call_target="tpu_custom_call" | custom-call | tf_op jit(solution)/shard_map/finish/pallas_call | solution.py:470
  (1 shorter events, 0.0 us)
Async XLA Ops:
  0.0 6.0 %copy-start.2 = (bf16[256,512]{1,0:T(8,128)(2,1)S(1)}, bf16[256,512]{1,0:T(8,128)(2,1)}, u32[]{:S(2)}) copy-start(bf16[256,512]{1,0:T(8,128)(2,1)} %wp_ref.1) | copy-start | bytes 786436
  0.0 6.0 %copy-start.3 = (bf16[4,8,512]{2,1,0:T(8,128)(2,1)S(1)}, bf16[4,8,512]{2,1,0:T(8,128)(2,1)}, u32[]{:S(2)}) copy-start(bf16[4,8,512]{2,1,0:T(8,128)(2,1)} %param.19) | copy-start | bytes 98308
  5.4 2.3 %collective-permute-start = (f32[32,512]{1,0:T(8,128)S(1)}, f32[32,512]{1,0:T(8,128)S(1)}, u32[]{:S(2)}, u32[]{:S(2)}) collective-permute-start(f32[32,512]{1,0:T(8,128)S(1)} %get-tuple-element.27.after_ref.mine_ref), channel_id=1, source_target_pairs={{0,1},{1,0},{2,3},{3,2},{4,5},{5,4},{6,7},{7,6},{8,9},{9,8},{10,11... | collective-permute-start | bytes 196616 | tf_op jit(solution)/shard_map/ppermute | solution.py:507
  6.0 1.8 %copy-start = (bf16[512,256]{1,0:T(8,128)(2,1)S(1)}, bf16[512,256]{1,0:T(8,128)(2,1)}, u32[]{:S(2)}) copy-start(bf16[512,256]{1,0:T(8,128)(2,1)} %wq_ref.3) | copy-start | bytes 786436
  6.0 1.8 %copy-start.1 = (bf16[512,256]{1,0:T(8,128)(2,1)S(1)}, bf16[512,256]{1,0:T(8,128)(2,1)}, u32[]{:S(2)}) copy-start(bf16[512,256]{1,0:T(8,128)(2,1)} %wg_ref.3) | copy-start | bytes 786436
  6.0 20.2 %copy-start.4 = (s32[4,128]{1,0:T(4,128)S(1)}, s32[4,128]{1,0:T(4,128)}, u32[]{:S(2)}) copy-start(s32[4,128]{1,0:T(4,128)} %cutoff_ref.1) | copy-start | bytes 6148
  71.7 1.3 %collective-permute-start.1 = (f32[32,512]{1,0:T(8,128)S(1)}, f32[32,512]{1,0:T(8,128)S(1)}, u32[]{:S(2)}, u32[]{:S(2)}) collective-permute-start(f32[32,512]{1,0:T(8,128)S(1)} %embed_grads.1.mine_ref), channel_id=1, source_target_pairs={{0,1},{1,0},{2,3},{3,2},{4,5},{5,4},{6,7},{7,6},{8,9},{9,8},{10,11... | collective-permute-start | bytes 196616 | tf_op jit(solution)/shard_map/ppermute | solution.py:520
  75.1 2.2 %collective-permute-start.2 = (bf16[64,1024]{1,0:T(8,128)(2,1)S(1)}, bf16[64,1024]{1,0:T(8,128)(2,1)S(1)}, u32[]{:S(2)}, u32[]{:S(2)}) collective-permute-start(bf16[64,1024]{1,0:T(8,128)(2,1)S(1)} %get-tuple-element.45), channel_id=1, source_target_pairs={{0,1},{1,0},{2,3},{3,2},{4,5},{5,4},{6,7},{7,6},{8,9},{9,8},{10,11... | collective-permute-start | bytes 393224 | tf_op jit(solution)/shard_map/ppermute | solution.py:522
  76.9 1.4 %collective-permute-start.3 = (bf16[64,1024]{1,0:T(8,128)(2,1)S(1)}, bf16[64,1024]{1,0:T(8,128)(2,1)S(1)}, u32[]{:S(2)}, u32[]{:S(2)}) collective-permute-start(bf16[64,1024]{1,0:T(8,128)(2,1)S(1)} %get-tuple-element.48), channel_id=1, source_target_pairs={{0,1},{1,0},{2,3},{3,2},{4,5},{5,4},{6,7},{7,6},{8,9},{9,8},{10,11... | collective-permute-start | bytes 393224 | tf_op jit(solution)/shard_map/ppermute | solution.py:525

commit v6 on v5

--- a/solution.py
+++ b/solution.py
@@ -352,19 +352,21 @@
     )(grads, kept_in_vmem(slopes), *map(kept_in_vmem, history))
 
 
-def embed_kernel(parts_ref, gg_ref, qs_ref, gs_ref, wq_ref, wg_ref, out_ref):
+def embed_kernel(parts_ref, gg_ref, qs_ref, gs_ref, wq_ref, wg_ref, out_ref, send_ref):
     total = parts_ref[0].astype(F32)
     for index in range(1, parts_ref.shape[0]):
         total = total + parts_ref[index].astype(F32)
     query_back = (total.reshape(qs_ref.shape) * qs_ref[...]).astype(BF16)
     gate_back = (gg_ref[...] * gs_ref[...]).astype(BF16)
-    out_ref[...] = contract_last(query_back, wq_ref[...]) + contract_last(gate_back, wg_ref[...])
+    part = contract_last(query_back, wq_ref[...]) + contract_last(gate_back, wg_ref[...])
+    out_ref[...] = part
+    send_ref[...] = part.astype(BF16)
 
 
 def embed_grads(partials, gate_grad, query_slope, gate_slope, w_query, w_gate):
     return pl.pallas_call(
         embed_kernel,
-        out_shape=jax.ShapeDtypeStruct((gate_grad.shape[0], w_query.shape[0]), F32),
+        out_shape=[jax.ShapeDtypeStruct((gate_grad.shape[0], w_query.shape[0]), kind) for kind in (F32, BF16)],
         compiler_params=params(8),
         name="embed_grads",
     )(partials, gate_grad, query_slope, gate_slope, w_query, w_gate)
@@ -373,7 +375,7 @@
 def content_first_kernel(parts, block, mine_ref, other_ref, we_ref, slope_ref, wh_ref, keep_ref, send_ref, back_ref):
     count = mine_ref.shape[0]
     half = parts // 2
-    embed_grad = (0.5 * (mine_ref[...] + other_ref[...])).astype(BF16)
+    embed_grad = (0.5 * (mine_ref[...] + other_ref[...].astype(F32))).astype(BF16)
     hidden_grad = 0.5 * contract_last(embed_grad, we_ref[...])
     head = lax.axis_index("head")
     for index in range(parts):
@@ -395,12 +397,12 @@
 
 
 def content_second_kernel(block, back_ref, wh_ref, keep_ref, send_ref):
-    content_columns(wh_ref.shape[0] // 2, block, back_ref, wh_ref, keep_ref, send_ref)
-
-
-def content_first(mine, other, w_embed, slopes, w_hidden, parts, block):
+    content_columns(wh_ref.shape[0] - keep_ref.shape[1], block, back_ref, wh_ref, keep_ref, send_ref)
+
+
+def content_first(mine, other, w_embed, slopes, w_hidden, parts, block, early):
     count, hidden = slopes.shape
-    shape = (count // 2, w_hidden.shape[0] // 2)
+    shape = (count // 2, early)
     return pl.pallas_call(
         functools.partial(content_first_kernel, parts, block),
         in_specs=in_vmem(5),
@@ -415,8 +417,8 @@
     )(mine, other, kept_in_vmem(w_embed), kept_in_vmem(slopes), kept_in_vmem(w_hidden))
 
 
-def content_second(back, w_hidden, block):
-    shape = (back.shape[0] // 2, w_hidden.shape[0] // 2)
+def content_second(back, w_hidden, block, early):
+    shape = (back.shape[0] // 2, w_hidden.shape[0] - early)
     return pl.pallas_call(
         functools.partial(content_second_kernel, block),
         in_specs=in_vmem(2),
@@ -455,11 +457,11 @@
 
 
 def finish_kernel(first_ref, keep_ref, got_ref, out_hbm, last_ref, sems):
-    width = first_ref.shape[2]
+    width, rest = first_ref.shape[2], last_ref.shape[2]
     early = pltpu.make_async_copy(first_ref, out_hbm.at[:, :, pl.ds(0, width)], sems.at[0])
     early.start()
     last_ref[...] = placed_rows(keep_ref, got_ref, *first_ref.shape[:2])
-    late = pltpu.make_async_copy(last_ref, out_hbm.at[:, :, pl.ds(width, width)], sems.at[1])
+    late = pltpu.make_async_copy(last_ref, out_hbm.at[:, :, pl.ds(width, rest)], sems.at[1])
     late.start()
     early.wait()
     late.wait()
@@ -467,12 +469,13 @@
 
 def finish(first, keep, got):
     count, half, width = first.shape
+    rest = keep.shape[1]
     return pl.pallas_call(
         finish_kernel,
         in_specs=in_vmem(3),
         out_specs=pl.BlockSpec(memory_space=pltpu.HBM),
-        out_shape=jax.ShapeDtypeStruct((count, half, 2 * width), BF16),
-        scratch_shapes=[pltpu.VMEM(first.shape, BF16), pltpu.SemaphoreType.DMA((2,))],
+        out_shape=jax.ShapeDtypeStruct((count, half, width + rest), BF16),
+        scratch_shapes=[pltpu.VMEM((count, half, rest), BF16), pltpu.SemaphoreType.DMA((2,))],
         compiler_params=params(8),
         name="finish",
     )(kept_in_vmem(first), keep, got)
@@ -516,11 +519,12 @@
     sends, gate_grad = norm_grads(to_owner(partial), normed_grad, out_grad, heads)
     history = (first_keys, first_values, rest_keys, rest_values)
     partial = backward_attention(to_owner(sends), slopes, history, heads)
-    mine = embed_grads(to_owner(partial), gate_grad, query_slope, gate_slope, w_query, w_gate)
-    other = lax.ppermute(mine, "head", swap)
-    keep1, send1, back = content_first(mine, other, w_embed, hidden_slope, w_hidden, parts, 256)
+    mine, send = embed_grads(to_owner(partial), gate_grad, query_slope, gate_slope, w_query, w_gate)
+    other = lax.ppermute(send, "head", swap)
+    early = width * 5 // 8
+    keep1, send1, back = content_first(mine, other, w_embed, hidden_slope, w_hidden, parts, 256, early)
     got1 = lax.ppermute(send1, "head", swap)
-    keep2, send2 = content_second(back, w_hidden, 256)
+    keep2, send2 = content_second(back, w_hidden, 256, early)
     half = parts // head_count
     got2 = lax.ppermute(send2, "head", swap)
     first = place(keep1, got1, count, half)

time: 79.7 us -> 79.5 us (level)
    ppermute x2 -> x1, waiting for transfers between devices: 1.26 us -> 0.01 us  [body(): other = lax.ppermute(mine, 'head', swap)]
    ppermute x0 -> x1, waiting for transfers between devices: none -> 1.19 us  [body(): other = lax.ppermute(send, 'head', swap)]
where the time goes in v6:
time: 79.5 us; the launch traced here: 79.1 us
  blocking collectives  56.2 us (71%)
  Pallas kernels  19.6 us (25%)
  waiting for transfers between devices  1.85 us (2%)
  starting transfers between devices  1.23 us (2%)
    all_to_all x4, blocking collectives, to_owner(): return lax.all_to_all(blocks, 'ctx', 0, 0, tiled=True)  56.2 us
    pallas_call x1, Pallas kernels, encode(): pl.pallas_call(functools.partial(encode_kernel, parts, block, 4), in_spec...  5.39 us
    pallas_call x1, Pallas kernels, forward_attention(): pl.pallas_call(functools.partial(forward_kernel, heads, *chunks_of(events...  4.37 us
    pallas_call x1, Pallas kernels, backward_attention(): pl.pallas_call(functools.partial(backward_kernel, DH ** (-0.5), heads, *c...  2.67 us
    pallas_call x1, Pallas kernels, content_first(): pl.pallas_call(functools.partial(content_first_kernel, parts, block), in_...  2.39 us
    pallas_call x1, Pallas kernels, warm(): pl.pallas_call(warm_kernel, in_specs=in_vmem(3) + [pl.BlockSpec(memory_sp...  1.71 us
  transfers between devices with their start and end apart: 4, of which 2 were waited for; matrix products, arithmetic and copies ran while one was open for 0% of the time, Pallas kernels for 4%

profile of v6, /device:TPU:0, one launch (start us, length us, event | category | flops | bytes accessed | tf_op | source)
XLA Modules:
  0.0 79.1 jit_solution(4222511176028958313)
XLA Ops:
  0.0 0.0 copy-start.2
  0.0 0.0 copy-start.3
  0.0 5.4 %encode.1 = (f32[128,2048]{1,0:T(8,128)S(1)}, f32[32,512]{1,0:T(8,128)S(1)}, bf16[2048,2048]{1,0:T(8,128)(2,1)S(1)}, bf16[2048,512]{1,0:T(8,128)(2,1)S(1)}) custom-call(bf16[32,4,2048]{2,1,0:T(4,128)(2,1)} %bitcast.4, bf16[2048,2048]{1,0:T(8,128)(2,1)} %wh_hbm.1, bf16[2048,512]{1,0:T(8,128)(2,1)} %we_hbm.1), custom_call_target="tpu_custom_call" | custom-call | tf_op jit(solution)/shard_map/encode/pallas_call | solution.py:109
  5.4 0.6 collective-permute-start
  6.0 0.0 copy-done.2
  6.0 0.0 copy-done.3
  6.0 0.0 copy-start
  6.0 0.0 copy-start.4
  6.0 1.7 %warm.1 = (f32[32,256]{1,0:T(8,128)S(1)}, bf16[2304,256]{1,0:T(8,128)(2,1)S(1)}, bf16[2304,256]{1,0:T(8,128)(2,1)S(1)}) custom-call(f32[32,512]{1,0:T(8,128)S(1)} %get-tuple-element.29.after_ref.mine_ref, bf16[32,512]{1,0:T(8,128)(2,1)S(1)} %bitcast.3, bf16[256,512]{1,0:T(8,128)(2,1)S(1)} %copy-done.2, bf16[4,2304,256]{2,1,0:T(8,128)(2,1)} %key_hbm.3, ...), custom_call_target="tpu_custom_call" | custom-call | tf_op jit(solution)/shard_map/warm/pallas_call | solution.py:143
  7.7 0.0 collective-permute-done.other_ref
  7.7 0.0 copy-done
  7.7 0.0 copy-done.1
  7.7 0.2 project.1
  8.0 18.2 %all_to_all.20.query_ref = bf16[16,4,8,256]{3,2,1,0:T(8,128)(2,1)S(1)} all-to-all(bf16[16,4,8,256]{3,2,1,0:T(8,128)(2,1)S(1)} %get-tuple-element.31), channel_id=1, replica_groups=mesh['ctx'=16,'head'=2] {'ctx'}, dimensions={0} | all-to-all | bytes 524288 | tf_op jit(solution)/shard_map/all_to_all | solution.py:505
  26.2 0.0 copy-done.4
  26.2 4.4 %attention_forward.1 = (bf16[16,4,8,256]{3,2,1,0:T(8,128)(2,1)S(1)}, bf16[4,2,128,2304]{3,2,1,0:T(8,128)(2,1)S(1)}, bf16[3,2304,256]{2,1,0:T(8,128)(2,1)S(1)}, bf16[3,2304,256]{2,1,0:T(8,128)(2,1)S(1)}) custom-call(bf16[16,4,8,256]{3,2,1,0:T(8,128)(2,1)S(1)} %all_to_all.20.query_ref, s32[4,128]{1,0:T(4,128)S(1)} %copy-done.4, ...), custom_call_target="tpu_custom_call" | custom-call | tf_op jit(solution)/shard_map/attention_forward/pallas_call | solution.py:256
  30.5 12.8 %all_to_all.21.parts_ref = bf16[16,4,8,256]{3,2,1,0:T(8,128)(2,1)S(1)} all-to-all(bf16[16,4,8,256]{3,2,1,0:T(8,128)(2,1)S(1)} %get-tuple-element.34), channel_id=1, replica_groups=mesh['ctx'=16,'head'=2] {'ctx'}, dimensions={0} | all-to-all | bytes 524288 | tf_op jit(solution)/shard_map/all_to_all | solution.py:505
  43.4 0.2 norm_grads.1
  43.6 12.6 %all_to_all.22.grad_ref = bf16[16,4,8,256]{3,2,1,0:T(8,128)(2,1)S(1)} all-to-all(bf16[16,4,8,256]{3,2,1,0:T(8,128)(2,1)S(1)} %get-tuple-element.36), channel_id=1, replica_groups=mesh['ctx'=16,'head'=2] {'ctx'}, dimensions={0} | all-to-all | bytes 524288 | tf_op jit(solution)/shard_map/all_to_all | solution.py:505
  56.2 2.7 %attention_backward.1 = bf16[16,4,8,256]{3,2,1,0:T(8,128)(2,1)S(1)} custom-call(bf16[16,4,8,256]{3,2,1,0:T(8,128)(2,1)S(1)} %all_to_all.22.grad_ref, bf16[4,2,128,2304]{3,2,1,0:T(8,128)(2,1)S(1)} %get-tuple-element.37.slope_ref, bf16[2304,256]{1,0:T(8,128)(2,1)S(1)} %get-tuple-element.32.first_key_ref, ...), custom_call_target="tpu_custom_call" | custom-call | tf_op jit(solution)/shard_map/attention_backward/pallas_call | solution.py:345
  58.9 12.5 %all_to_all.23.parts_ref = bf16[16,4,8,256]{3,2,1,0:T(8,128)(2,1)S(1)} all-to-all(bf16[16,4,8,256]{3,2,1,0:T(8,128)(2,1)S(1)} %attention_backward.1), channel_id=1, replica_groups=mesh['ctx'=16,'head'=2] {'ctx'}, dimensions={0} | all-to-all | bytes 524288 | tf_op jit(solution)/shard_map/all_to_all | solution.py:505
  71.4 0.2 embed_grads.1
  71.7 0.0 collective-permute-start.1
  71.7 1.2 %collective-permute-done.1.other_ref = bf16[32,512]{1,0:T(8,128)(2,1)S(1)} collective-permute-done((bf16[32,512]{1,0:T(8,128)(2,1)S(1)}, bf16[32,512]{1,0:T(8,128)(2,1)S(1)}, u32[]{:S(2)}, u32[]{:S(2)}) %collective-permute-start.1) | collective-permute-done | bytes 32800 | tf_op jit(solution)/shard_map/ppermute | solution.py:523
  72.9 2.4 %content_first.1 = (f32[64,1280]{1,0:T(8,128)S(1)}, bf16[64,1280]{1,0:T(8,128)(2,1)S(1)}, bf16[128,2048]{1,0:T(8,128)(2,1)S(1)}) custom-call(f32[32,512]{1,0:T(8,128)S(1)} %get-tuple-element.43.mine_ref, bf16[32,512]{1,0:T(8,128)(2,1)S(1)} %collective-permute-done.1.other_ref, bf16[2048,512]{1,0:T(8,128)(2,1)S(1)} %get-tuple-element.45.we_ref, ...), custom_call_target="tpu_custom_call" | custom-call | tf_op jit(solution)/shard_map/content_first/pallas_call | solution.py:406
  75.3 0.2 collective-permute-start.2
  75.5 1.2 %content_second.1 = (f32[64,768]{1,0:T(8,128)S(1)}, bf16[64,768]{1,0:T(8,128)(2,1)S(1)}) custom-call(bf16[128,2048]{1,0:T(8,128)(2,1)S(1)} %get-tuple-element.50.back_ref, bf16[2048,2048]{1,0:T(8,128)(2,1)S(1)} %get-tuple-element.47.wh_ref), custom_call_target="tpu_custom_call" | custom-call | tf_op jit(solution)/shard_map/content_second/pallas_call | solution.py:422
  76.7 0.4 collective-permute-start.3
  77.1 0.0 collective-permute-done.2.got_ref
  77.1 0.3 place.1.first_ref
  77.4 0.7 collective-permute-done.3.got_ref
  78.1 0.9 %finish.1 = bf16[32,2,2048]{2,1,0:T(2,128)(2,1)} custom-call(bf16[32,2,1280]{2,1,0:T(2,128)(2,1)S(1)} %place.1.first_ref, f32[64,768]{1,0:T(8,128)S(1)} %get-tuple-element.51.keep_ref, bf16[64,768]{1,0:T(8,128)(2,1)S(1)} %collective-permute-done.3.got_ref), custom_call_target="tpu_custom_call" | custom-call | tf_op jit(solution)/shard_map/finish/pallas_call | solution.py:473
  (1 shorter events, 0.0 us)
Async XLA Ops:
  0.0 6.0 %copy-start.2 = (bf16[256,512]{1,0:T(8,128)(2,1)S(1)}, bf16[256,512]{1,0:T(8,128)(2,1)}, u32[]{:S(2)}) copy-start(bf16[256,512]{1,0:T(8,128)(2,1)} %wp_ref.1) | copy-start | bytes 786436
  0.0 6.0 %copy-start.3 = (bf16[4,8,512]{2,1,0:T(8,128)(2,1)S(1)}, bf16[4,8,512]{2,1,0:T(8,128)(2,1)}, u32[]{:S(2)}) copy-start(bf16[4,8,512]{2,1,0:T(8,128)(2,1)} %param.19) | copy-start | bytes 98308
  5.4 2.3 %collective-permute-start = (f32[32,512]{1,0:T(8,128)S(1)}, f32[32,512]{1,0:T(8,128)S(1)}, u32[]{:S(2)}, u32[]{:S(2)}) collective-permute-start(f32[32,512]{1,0:T(8,128)S(1)} %get-tuple-element.29.after_ref.mine_ref), channel_id=1, source_target_pairs={{0,1},{1,0},{2,3},{3,2},{4,5},{5,4},{6,7},{7,6},{8,9},{9,8},{10,11... | collective-permute-start | bytes 196616 | tf_op jit(solution)/shard_map/ppermute | solution.py:510
  6.0 1.8 %copy-start = (bf16[512,256]{1,0:T(8,128)(2,1)S(1)}, bf16[512,256]{1,0:T(8,128)(2,1)}, u32[]{:S(2)}) copy-start(bf16[512,256]{1,0:T(8,128)(2,1)} %wq_ref.3) | copy-start | bytes 786436
  6.0 1.8 %copy-start.1 = (bf16[512,256]{1,0:T(8,128)(2,1)S(1)}, bf16[512,256]{1,0:T(8,128)(2,1)}, u32[]{:S(2)}) copy-start(bf16[512,256]{1,0:T(8,128)(2,1)} %wg_ref.3) | copy-start | bytes 786436
  6.0 20.2 %copy-start.4 = (s32[4,128]{1,0:T(4,128)S(1)}, s32[4,128]{1,0:T(4,128)}, u32[]{:S(2)}) copy-start(s32[4,128]{1,0:T(4,128)} %cutoff_ref.1) | copy-start | bytes 6148
  71.7 1.2 %collective-permute-start.1 = (bf16[32,512]{1,0:T(8,128)(2,1)S(1)}, bf16[32,512]{1,0:T(8,128)(2,1)S(1)}, u32[]{:S(2)}, u32[]{:S(2)}) collective-permute-start(bf16[32,512]{1,0:T(8,128)(2,1)S(1)} %get-tuple-element.44), channel_id=1, source_target_pairs={{0,1},{1,0},{2,3},{3,2},{4,5},{5,4},{6,7},{7,6},{8,9},{9,8},{10,11... | collective-permute-start | bytes 98312 | tf_op jit(solution)/shard_map/ppermute | solution.py:523
  75.3 1.8 %collective-permute-start.2 = (bf16[64,1280]{1,0:T(8,128)(2,1)S(1)}, bf16[64,1280]{1,0:T(8,128)(2,1)S(1)}, u32[]{:S(2)}, u32[]{:S(2)}) collective-permute-start(bf16[64,1280]{1,0:T(8,128)(2,1)S(1)} %get-tuple-element.49), channel_id=1, source_target_pairs={{0,1},{1,0},{2,3},{3,2},{4,5},{5,4},{6,7},{7,6},{8,9},{9,8},{10,11... | collective-permute-start | bytes 491528 | tf_op jit(solution)/shard_map/ppermute | solution.py:526
  76.7 1.4 %collective-permute-start.3 = (bf16[64,768]{1,0:T(8,128)(2,1)S(1)}, bf16[64,768]{1,0:T(8,128)(2,1)S(1)}, u32[]{:S(2)}, u32[]{:S(2)}) collective-permute-start(bf16[64,768]{1,0:T(8,128)(2,1)S(1)} %get-tuple-element.52), channel_id=1, source_target_pairs={{0,1},{1,0},{2,3},{3,2},{4,5},{5,4},{6,7},{7,6},{8,9},{9,8},{10,11... | collective-permute-start | bytes 294920 | tf_op jit(solution)/shard_map/ppermute | solution.py:529
